TPU v7x, 512 devices: a whole 4x8x8 slice. The times are simulated.
512 devices in a mesh: pipe: 8 (over z), ctx: 32 (over x, y_hi, core), tp: 2 (over y_lo).
Axes of the slice: x: 4, y: 8 (y_hi: 4, y_lo: 2; y = y_hi * 2 + y_lo), z: 8, core: 2. Of those that a mesh axis runs over, the one named last changes fastest.
Arguments:
- queries: bfloat16 [8, 2048, 128, 128], P('pipe', 'ctx', 'tp'), may hold values from -10 to 10
- span_keys: bfloat16 [8, 2048, 8, 128], P('pipe', 'ctx', 'tp'), may hold values from -6 to 6
- span_values: bfloat16 [8, 2048, 8, 128], P('pipe', 'ctx', 'tp'), may hold values from -12 to 12
- cache_keys: bfloat16 [8, 1024, 8, 128], P('pipe', 'ctx', 'tp'), may hold values from -6 to 6
- cache_values: bfloat16 [8, 1024, 8, 128], P('pipe', 'ctx', 'tp'), may hold values from -6 to 6
- scale_exps: int32 [8, 64, 8, 2], P('pipe', 'ctx', 'tp'), may hold values from -3 to 1
- block_order: int32 [8, 64], P('pipe'), may hold values from 0 to 63, each once within a row
Outputs:
- handed: bfloat16 [8, 2048, 128, 128], P('pipe', 'ctx', 'tp')
All inputs are finite; a program needn't handle non-finite values.
Results may differ from a plain program's by a relative error of at most 0.006.
Values may be sent and summed in bfloat16 or wider, within the bound.
No kernel may reach another device: no remote copies, remote signals or barrier semaphores. Data moves between devices by JAX's collectives and lax.ppermute only.
A program may use at most 128 MiB of HBM per device.

v0:
```python
import jax
import jax.numpy as jnp
from jax import lax
from jax.sharding import PartitionSpec as P

CBLK = 16


def shifted(value, axis, steps):
    count = lax.axis_size(axis)
    pairs = [(source, (source + steps) % count) for source in range(count)]
    return lax.ppermute(value, axis, pairs)


def hadamard(order):
    rows = jnp.arange(order, dtype=jnp.int32)[:, None]
    cols = jnp.arange(order, dtype=jnp.int32)[None, :]
    common = jnp.zeros((order, order), jnp.int32)
    for bit in range(order.bit_length() - 1):
        common = common + (jnp.right_shift(rows, bit) & 1) * (jnp.right_shift(cols, bit) & 1)
    signs = 1.0 - 2.0 * (common % 2).astype(jnp.float32)
    return signs * (1.0 / order**0.5)


def table_lookup(table, slots):
    match = jnp.arange(table.shape[0], dtype=jnp.int32)[None, :] == slots[:, None]
    return jnp.sum(jnp.where(match, table[None, :], 0), axis=1)


def attend(carry, block, grouped, pos_query, order, half, cache_len, rows_dev):
    best, total, accum = carry
    keys = block[:, :, 0, :]
    vals = block[:, :, 1, :]
    count = block.shape[0]
    global_row = jnp.arange(count, dtype=jnp.int32)
    owner = global_row // rows_dev
    local = global_row % rows_dev
    offset = jnp.maximum(local - cache_len, 0)
    pos_key = table_lookup(order, 2 * owner + offset // half) * half + offset % half
    visible = (local < cache_len)[None, :] | (pos_key[None, :] <= pos_query[:, None])
    inv = 1.0 / grouped.shape[-1] ** 0.5
    score = jnp.einsum("tgqd,kgd->gqtk", grouped, keys, preferred_element_type=jnp.float32) * inv
    score = jnp.where(visible[None, None], score, -jnp.inf)
    best_new = jnp.max(score, axis=-1)
    safe = jnp.where(best_new == -jnp.inf, 0.0, best_new)
    expo = jnp.exp(score - safe[..., None])
    rescale = jnp.exp(best - safe)
    total = total * rescale + jnp.sum(expo, axis=-1)
    accum = accum * rescale[..., None] + jnp.einsum(
        "gqtk,kgd->gqtd", expo.astype(jnp.bfloat16), vals, preferred_element_type=jnp.float32
    )
    return (best_new, total, accum)


def on_device(queries, span_keys, span_values, cache_keys, cache_values, scale_exps, block_order):
    mine = lax.axis_index("ctx")
    tok_local = queries.shape[1]
    head_local = queries.shape[2]
    kv_local = span_keys.shape[2]
    width = queries.shape[3]
    cache_len = cache_keys.shape[1]
    half = tok_local // 2
    rows_dev = cache_len + tok_local
    grouped = queries[0].reshape(tok_local, kv_local, head_local // kv_local, width)
    order = block_order[0]
    factor = jnp.repeat(jnp.exp2(scale_exps[0].astype(jnp.float32)), CBLK, axis=0)
    keys_ctx = (cache_keys[0].astype(jnp.float32) * factor[:, :, 0:1]).astype(jnp.bfloat16)
    vals_ctx = (cache_values[0].astype(jnp.float32) * factor[:, :, 1:2]).astype(jnp.bfloat16)
    own_keys = jnp.concatenate([keys_ctx, span_keys[0]], axis=0)
    own_vals = jnp.concatenate([vals_ctx, span_values[0]], axis=0)
    own_block = jnp.stack([own_keys, own_vals], axis=2)
    index = jnp.arange(tok_local, dtype=jnp.int32)
    pos_query = table_lookup(order, 2 * mine + index // half) * half + index % half
    group_size = head_local // kv_local
    initial = (
        jnp.full((kv_local, group_size, tok_local), -jnp.inf, jnp.float32),
        jnp.zeros((kv_local, group_size, tok_local), jnp.float32),
        jnp.zeros((kv_local, group_size, tok_local, width), jnp.float32),
    )
    carry = attend(
        initial,
        lax.all_gather(own_block, "ctx", axis=0, tiled=True),
        grouped,
        pos_query,
        order,
        half,
        cache_len,
        rows_dev,
    )
    best, total, accum = carry
    mixed = accum / total[..., None]
    rotated = jnp.dot(mixed.reshape(-1, width), hadamard(width))
    rotated = rotated.reshape(kv_local, group_size, tok_local, width).transpose(2, 0, 1, 3)
    result = rotated.reshape(1, tok_local, head_local, width).astype(jnp.bfloat16)
    return shifted(result, "pipe", 1)


def solution(mesh):
    placed = (
        P("pipe", "ctx", "tp", None),
        P("pipe", "ctx", "tp", None),
        P("pipe", "ctx", "tp", None),
        P("pipe", "ctx", "tp", None),
        P("pipe", "ctx", "tp", None),
        P("pipe", "ctx", "tp", None),
        P("pipe", None),
    )
    return jax.shard_map(
        on_device,
        mesh=mesh,
        in_specs=placed,
        out_specs=P("pipe", "ctx", "tp", None),
        check_vma=False,
    )
```

profile of v0, /device:TPU:1, one launch (start us, length us, event | category | flops | bytes accessed | tf_op | source)
XLA Modules:
  0.0 190.2 jit_solution(14502393834735405781)
XLA Ops:
  6.5 0.0 copy-start
  6.5 0.0 all-gather.2.cloned.1.call-start
  6.5 0.8 exponential_bitcast_fusion
  7.3 0.1 copy.16
  7.4 0.1 broadcast_in_dim.66
  7.5 0.1 reshape.263
  7.6 0.9 copy.34
  8.4 0.9 copy.33
  9.3 0.9 fusion.29
  10.2 0.7 pad_maximum_fusion
  10.9 0.0 all-gather.2.cloned.1.call-update
  11.0 0.8 select_reduce_fusion.1
  11.9 0.9 select_reduce_fusion
  12.8 0.2 compare_or_fusion
  13.0 78.2 %all-gather.2.cloned.1.call-done = bf16[3072,4,2,128]{3,0,1,2:T(8,128)(2,1)} async-done(((bf16[96,4,2,128]{3,0,1,2:T(8,128)(2,1)}), bf16[3072,4,2,128]{3,0,1,2:T(8,128)(2,1)}) %all-gather.2.cloned.1.call-update) | async-done | bytes 6291472 | tf_op jit(solution)/shard_map/all_gather | solution.py:82
  91.2 0.0 copy-done
  91.2 20.1 %fusion.2 = (f32[4,16,64]{2,1,0:T(8,128)S(1)}, f32[4,3072,64,16]{1,2,3,0:T(8,128)}) fusion(pred[64,3072]{1,0:T(8,128)(4,1)S(1)} %compare_or_fusion, bf16[64,4,16,128]{3,2,1,0:T(8,128)(2,1)S(1)} %bitcast.69, bf16[3072,4,2,128]{3,0,1,2:T(8,128)(2,1)} %all-gather.2.cloned.1.call-done), kind=kOutput, calls=%fused_computation.4 | convolution fusion | flops 3258970112 | bytes 54738944 | tf_op jit(solution)/shard_map/tgqd,kgd->gqtk/dot_general | solution.py:42
  111.4 21.7 %fusion = f32[4,16,64]{2,1,0:T(8,128)S(1)} fusion(f32[4,3072,64,16]{1,2,3,0:T(8,128)} %get-tuple-element.10, f32[4,16,64]{2,1,0:T(8,128)S(1)} %compare_select_fusion, pred[64,3072]{1,0:T(8,128)(4,1)S(1)} %compare_or_fusion), kind=kLoop, calls=%fused_computation.2 | loop fusion | flops 50327552 | bytes 50561024 | tf_op jit(solution)/shard_map/reduce_sum | solution.py:48
  133.1 19.8 %fusion.14 = bf16[4,16,64,128]{3,2,1,0:T(8,128)(2,1)S(1)} fusion(bf16[3072,4,2,128]{3,0,1,2:T(8,128)(2,1)} %all-gather.2.cloned.1.call-done, f32[4,3072,64,16]{1,2,3,0:T(8,128)} %get-tuple-element.10, f32[4,16,64]{2,1,0:T(8,128)S(1)} %compare_select_fusion, pred[64,3072]{1,0:T(8,128)(4,1)S(1)} %compare_or_fusion, f32[4,16,64]{2,1,0:T(8,128)S(1)} %get-tuple-element.6, ...), kind=kOutput, calls=%fused_computation.13 | convolution fusion | flops 3407806464 | bytes 54828032 | tf_op jit(solution)/shard_map/dot_general | solution.py:92
  152.9 0.7 copy.21
  153.5 3.3 %collective-permute-start = (bf16[1,64,64,128]{3,2,1,0:T(8,128)(2,1)S(1)}, bf16[1,64,64,128]{3,2,1,0:T(8,128)(2,1)S(1)}, u32[]{:S(2)}, u32[]{:S(2)}) collective-permute-start(bf16[1,64,64,128]{3,2,1,0:T(8,128)(2,1)S(1)} %copy.21), channel_id=1, source_target_pairs={{0,64},{64,128},{128,192},{192,256},{256,320},{320,384},{384,448},... | collective-permute-start | bytes 3145736 | tf_op jit(solution)/shard_map/ppermute | solution.py:12
  156.8 25.6 %collective-permute-done = bf16[1,64,64,128]{3,2,1,0:T(8,128)(2,1)S(1)} collective-permute-done((bf16[1,64,64,128]{3,2,1,0:T(8,128)(2,1)S(1)}, bf16[1,64,64,128]{3,2,1,0:T(8,128)(2,1)S(1)}, u32[]{:S(2)}, u32[]{:S(2)}) %collective-permute-start) | collective-permute-done | bytes 1048608 | tf_op jit(solution)/shard_map/ppermute | solution.py:12
  182.4 1.0 copy.36
  (14 shorter events, 0.1 us)
Async XLA Ops:
  6.5 84.7 %copy-start = (bf16[1,64,64,128]{3,2,1,0:T(8,128)(2,1)S(1)}, bf16[1,64,64,128]{3,2,1,0:T(8,128)(2,1)}, u32[]{:S(2)}) copy-start(bf16[1,64,64,128]{3,2,1,0:T(8,128)(2,1)} %param.7) | copy-start | bytes 3145732
  6.5 84.7 %all-gather.2.cloned.1.call-start = ((), (), s32[]{:S(2)}) async-start(), calls=%async_computation | async-start | bytes 6488064 | tf_op jit(solution)/shard_map/all_gather | solution.py:82
  153.5 28.8 %collective-permute-start = (bf16[1,64,64,128]{3,2,1,0:T(8,128)(2,1)S(1)}, bf16[1,64,64,128]{3,2,1,0:T(8,128)(2,1)S(1)}, u32[]{:S(2)}, u32[]{:S(2)}) collective-permute-start(bf16[1,64,64,128]{3,2,1,0:T(8,128)(2,1)S(1)} %copy.21), channel_id=1, source_target_pairs={{0,64},{64,128},{128,192},{192,256},{256,320},{320,384},{384,448},... | collective-permute-start | bytes 3145736 | tf_op jit(solution)/shard_map/ppermute | solution.py:12
Sparse Core Ops, SparseCore 0:
  11.1 80.1 all-gather.1
where the time goes:
time: 191 us; the launch traced here: 190 us
  waiting for transfers between devices  104 us (54%)
  matrix products  39.9 us (21%)
  other arithmetic  26 us (14%)
  between operations  13.5 us (7%)
  local copies, waits for them, and re-layouts  3.63 us (2%)
  starting transfers between devices  3.28 us (2%)
    all_gather x1, waiting for transfers between devices, on_device(): lax.all_gather(own_block, 'ctx', axis=0, tiled=True)  78.2 us
    ppermute x1, waiting for transfers between devices, shifted(): return lax.ppermute(value, axis, pairs)  25.6 us
    reduce_sum x1, other arithmetic, attend(): total = total * rescale + jnp.sum(expo, axis=-1)  21.7 us
    dot_general x1, matrix products, attend(): jnp.einsum('tgqd,kgd->gqtk', grouped, keys, preferred_element_type=jnp.fl...  20.1 us
    dot_general x1, matrix products, on_device(): rotated = jnp.dot(mixed.reshape(-1, width), hadamard(width))  19.8 us
  transfers between devices with their start and end apart: 2, of which 2 were waited for; matrix products, arithmetic and copies ran while one was open for 1% of the time, Pallas kernels for 0%

commit v1 on v0

v1 whole, which is shorter than its diff:
```python
import functools
import math

import jax
import jax.numpy as jnp
from jax import lax
from jax.experimental import pallas as pl
from jax.experimental.pallas import tpu as pltpu
from jax.sharding import Mesh, PartitionSpec as P


CBLK = 16
HALF = 32
HD = 128
GROUP = 16
FAR = -(2.0**100)
FLAT = ("pipe", "x", "y", "core")


def moved(value, sizes, dz=0, dx=0, dc=0):
    nz, nx, ny, nc = sizes
    pairs = []
    for z in range(nz):
        for x in range(nx):
            for y in range(ny):
                for c in range(nc):
                    source = ((z * nx + x) * ny + y) * nc + c
                    target = ((((z + dz) % nz) * nx + (x + dx) % nx) * ny + y) * nc + (c ^ dc)
                    pairs.append((source, target))
    return lax.ppermute(value, FLAT, pairs)


def iota(shape, axis):
    return lax.broadcasted_iota(jnp.int32, shape, axis)


def pick(rows, width, first, per_head, heads, scale=None):
    out = iota((rows, width), 0)
    src = iota((rows, width), 1)
    head = first + out // per_head
    token = out % per_head
    hit = src == token * heads + head
    if scale is None:
        return jnp.where(hit, 1.0, 0.0).astype(jnp.bfloat16)
    return jnp.where(hit, scale(token // CBLK, head), 0.0).astype(jnp.bfloat16)


def pack_body(core_ref, exps_ref, sk_ref, sv_ref, ck_ref, cv_ref, own_ref, other_ref, *, heads):
    core = core_ref[0]
    tok = sk_ref.shape[0] // heads
    cache = ck_ref.shape[0] // heads
    for which, ref in ((0, own_ref), (1, other_ref)):
        first = 2 * (core if which == 0 else 1 - core)
        span_pick = pick(2 * tok, heads * tok, first, tok, heads)
        for kv, (span, cached) in enumerate(((sk_ref, ck_ref), (sv_ref, cv_ref))):

            def scale(block, head):
                value = jnp.ones(block.shape, jnp.float32)
                for b in range(cache // CBLK):
                    for h in range(heads):
                        power = (jnp.int32(1) << (exps_ref[b, kv, h] + 3)).astype(jnp.float32) * 0.125
                        value = jnp.where((block == b) & (head == h), power, value)
                return value

            cache_pick = pick(2 * cache, heads * cache, first, cache, heads, scale)
            moved_span = jnp.dot(span_pick, span[...], preferred_element_type=jnp.float32).astype(jnp.bfloat16)
            moved_cache = jnp.dot(cache_pick, cached[...], preferred_element_type=jnp.float32).astype(jnp.bfloat16)
            for h in range(2):
                ref[h, kv, :cache] = moved_cache[h * cache : (h + 1) * cache]
                ref[h, kv, cache:] = moved_span[h * tok : (h + 1) * tok]


def pack(core, exps, span_keys, span_values, cache_keys, cache_values):
    tok, heads, width = span_keys.shape
    cache = cache_keys.shape[0]
    flat = lambda a: a.reshape(-1, width)
    shape = jax.ShapeDtypeStruct((2, 2, cache + tok, width), jnp.bfloat16)
    smem = pl.BlockSpec(memory_space=pltpu.SMEM)
    vmem = pl.BlockSpec(memory_space=pltpu.VMEM)
    return pl.pallas_call(
        functools.partial(pack_body, heads=heads),
        out_shape=(shape, shape),
        in_specs=[smem, smem, vmem, vmem, vmem, vmem],
        out_specs=(vmem, vmem),
        compiler_params=pltpu.CompilerParams(vmem_limit_bytes=8 << 20),
        name="pack_kv",
    )(core, exps, flat(span_keys), flat(span_values), flat(cache_keys), flat(cache_values))


def fill(place_ref, order_ref, chunk_refs, spots, ka, va, head_slot, tok, cache):
    x, y, core = place_ref[0], place_ref[1], place_ref[2]
    nx, ny = place_ref[3], place_ref[4]
    halves = tok // HALF
    lane = iota((HALF, HD), 1)
    within = iota((HALF, HD), 0)
    slot = lane // HALF
    base = jnp.zeros((HALF, HD), jnp.int32)
    for s in range(2 * halves):
        owner = (x * ny + y) * 2 + (core if s < halves else 1 - core)
        base = jnp.where(slot == s, order_ref[0, owner * halves + s % halves], base)
    pos_query = base * HALF + lane % HALF
    rows = cache + tok
    at = 0
    for ref, spot in zip(chunk_refs, spots):
        count = ref.shape[0]
        shift, first_y = spot
        src_x = (x + shift) % nx
        for k in range(count):
            for cc in range(2):
                owner = (src_x * ny + first_y + k) * 2 + (core if cc == 0 else 1 - core)
                ka[at : at + rows, :HD] = ref[k, cc, head_slot, 0]
                va[at : at + rows, :HD] = ref[k, cc, head_slot, 1]
                ka[at : at + cache, HD:] = jnp.zeros((cache, HD), jnp.bfloat16)
                for b in range(halves):
                    pos_key = order_ref[0, owner * halves + b] * HALF + within
                    start = at + cache + b * HALF
                    ka[start : start + HALF, HD:] = jnp.where(pos_key <= pos_query, 0.0, FAR).astype(jnp.bfloat16)
                at += rows
    va[:, HD:] = jnp.ones((va.shape[0], HD), jnp.bfloat16)


def stage_body(*refs, nq, nchunk, spots, first, last, tok, cache, tile_tok, sub):
    place_ref, order_ref = refs[0], refs[1]
    refs = refs[2:]
    q_refs, refs = refs[:nq], refs[nq:]
    chunk_refs, refs = refs[:nchunk], refs[nchunk:]
    if not first:
        (acc_in, max_in), refs = refs[:2], refs[2:]
    if last:
        (own_ref, other_ref), refs = refs[:2], refs[2:]
    else:
        (acc_out, max_out), refs = refs[:2], refs[2:]
    ka, va = refs
    head = pl.program_id(0)
    tile = pl.program_id(1)

    @pl.when(tile == 0)
    def _():
        fill(place_ref, order_ref, chunk_refs, spots, ka, va, head, tok, cache)

    rows = tile_tok * GROUP
    factor = math.log2(math.e) / math.sqrt(HD)
    if last:
        i, j = iota((HD, HD), 0), iota((HD, HD), 1)
        bits = i & j
        bits = bits ^ (bits >> 4)
        bits = bits ^ (bits >> 2)
        bits = (bits ^ (bits >> 1)) & 1
        signs = (1.0 - 2.0 * bits.astype(jnp.float32)).astype(jnp.bfloat16)
        signs = jnp.concatenate([signs, signs], axis=0)
    for s in range(rows // sub):
        tok0 = s * sub // GROUP
        tok1 = (s + 1) * sub // GROUP
        part = q_refs[0][tok0:tok1].reshape(sub, HD)
        if nq == 2:
            other = q_refs[1][tok0:tok1].reshape(sub, HD)
            part = jnp.where(tile < tok // tile_tok, part, other)
        token = tile * tile_tok + tok0 + iota((sub, HD), 0) // GROUP
        hot = jnp.where(iota((sub, HD), 1) == token, 1.0, 0.0).astype(jnp.bfloat16)
        left = jnp.concatenate([part, hot], axis=1)
        score = lax.dot_general(left, ka[...], (((1,), (1,)), ((), ())), preferred_element_type=jnp.float32)
        top = jnp.max(score, axis=1, keepdims=True)
        span = slice(s * sub, (s + 1) * sub)
        if not first:
            top_old = max_in[0, span, :1]
            top = jnp.maximum(top, top_old)
        weight = jnp.exp2((score - top) * factor).astype(jnp.bfloat16)
        acc = jnp.dot(weight, va[...], preferred_element_type=jnp.float32)
        if not first:
            acc = acc + acc_in[0, span] * jnp.exp2((top_old - top) * factor)
        if last:
            mixed = acc[:, :HD] / (acc[:, HD:] * math.sqrt(HD))
            high = mixed.astype(jnp.bfloat16)
            low = (mixed - high.astype(jnp.float32)).astype(jnp.bfloat16)
            turned = jnp.dot(jnp.concatenate([high, low], axis=1), signs, preferred_element_type=jnp.float32)
            turned = turned.astype(jnp.bfloat16).reshape(sub // GROUP, GROUP, HD)

            @pl.when(tile < tok // tile_tok)
            def _():
                own_ref[tok0:tok1] = turned

            @pl.when(tile >= tok // tile_tok)
            def _():
                other_ref[tok0:tok1] = turned
        else:
            acc_out[0, span] = acc
            max_out[0, span] = jnp.broadcast_to(top, (sub, HD))


def stage(place, order, queries, chunks, spots, state, tok, cache, last=False, tile_tok=64, sub=256):
    nq = len(queries)
    per = queries[0].shape[0] // tile_tok
    tiles = nq * per
    rows = tile_tok * GROUP
    total = 2 * tok * GROUP
    keys = sum(c.shape[0] for c in chunks) * 2 * (cache + tok)
    smem = pl.BlockSpec(memory_space=pltpu.SMEM)
    first = state is None
    in_specs = [smem]
    for n in range(nq):
        in_specs.append(pl.BlockSpec((tile_tok, GROUP, HD), lambda h, t, p, n=n: (jnp.clip(t - n * per, 0, per - 1), h, 0)))
    for c in chunks:
        in_specs.append(pl.BlockSpec(c.shape, lambda h, t, p, nd=c.ndim: (0,) * nd, pipeline_mode=pl.Buffered(1)))
    acc_spec = pl.BlockSpec((1, rows, 2 * HD), lambda h, t, p: (h, t, 0))
    max_spec = pl.BlockSpec((1, rows, HD), lambda h, t, p: (h, t, 0))
    operands = [order, *queries, *chunks]
    if not first:
        in_specs += [acc_spec, max_spec]
        operands += list(state)
    if last:
        out_specs = (
            pl.BlockSpec((tile_tok, GROUP, HD), lambda h, t, p: (jnp.minimum(t, per - 1), 2 * p[2] + h, 0)),
            pl.BlockSpec((tile_tok, GROUP, HD), lambda h, t, p: (jnp.maximum(t - per, 0), h, 0)),
        )
        out_shape = (
            jax.ShapeDtypeStruct((tok, 4 * GROUP, HD), jnp.bfloat16),
            jax.ShapeDtypeStruct((tok, 2 * GROUP, HD), jnp.bfloat16),
        )
    else:
        out_specs = (acc_spec, max_spec)
        out_shape = (
            jax.ShapeDtypeStruct((2, total, 2 * HD), jnp.float32),
            jax.ShapeDtypeStruct((2, total, HD), jnp.float32),
        )
    body = functools.partial(
        stage_body, nq=nq, nchunk=len(chunks), spots=spots, first=first, last=last, tok=tok, cache=cache,
        tile_tok=tile_tok, sub=sub,
    )
    return pl.pallas_call(
        body,
        grid_spec=pltpu.PrefetchScalarGridSpec(
            num_scalar_prefetch=1,
            grid=(2, tiles),
            in_specs=in_specs,
            out_specs=out_specs,
            scratch_shapes=[pltpu.VMEM((keys, 2 * HD), jnp.bfloat16), pltpu.VMEM((keys, 2 * HD), jnp.bfloat16)],
        ),
        out_shape=out_shape,
        compiler_params=pltpu.CompilerParams(vmem_limit_bytes=32 << 20),
        name="stage_last" if last else "stage",
    )(place, *operands)


def put_body(place_ref, part_ref, whole_ref, out_ref, sem):
    heads = part_ref.shape[1]
    copy = pltpu.make_async_copy(part_ref, out_ref.at[:, pl.ds((1 - place_ref[2]) * heads, heads)], sem)
    copy.start()
    copy.wait()


def put(place, part, whole):
    raw = pl.BlockSpec(memory_space=pl.ANY)
    return pl.pallas_call(
        put_body,
        out_shape=jax.ShapeDtypeStruct(whole.shape, whole.dtype),
        in_specs=[pl.BlockSpec(memory_space=pltpu.SMEM), raw, raw],
        out_specs=raw,
        scratch_shapes=[pltpu.SemaphoreType.DMA],
        input_output_aliases={2: 0},
        compiler_params=pltpu.CompilerParams(vmem_limit_bytes=1 << 20),
        name="put",
    )(place, part, whole)


def on_device(queries, span_keys, span_values, cache_keys, cache_values, scale_exps, block_order, sizes):
    return relay(queries, span_keys, span_values, cache_keys, cache_values, scale_exps, block_order, sizes)


def relay(queries, span_keys, span_values, cache_keys, cache_values, scale_exps, block_order, sizes):
    _, nx, ny, nc = sizes
    tok, heads, width = queries.shape[1:]
    cache = cache_keys.shape[1]
    core = lax.axis_index("core").astype(jnp.int32)
    place = jnp.stack([lax.axis_index("x").astype(jnp.int32), lax.axis_index("y").astype(jnp.int32), core, jnp.int32(nx), jnp.int32(ny)])
    exps = scale_exps[0].transpose(0, 2, 1)
    own, other = pack(core.reshape(1), exps, span_keys[0], span_values[0], cache_keys[0], cache_values[0])
    own = moved(own, sizes, dz=1)
    other = moved(other, sizes, dz=1, dc=1)
    order = moved(block_order, sizes, dz=1)
    half_heads = heads // 2
    q_own = lax.dynamic_slice_in_dim(queries[0], core * half_heads, half_heads, 1)
    q_other = lax.dynamic_slice_in_dim(queries[0], (1 - core) * half_heads, half_heads, 1)
    q_own = moved(q_own, sizes, dz=1)
    q_other = moved(q_other, sizes, dz=1, dc=1)
    rows = 2 * 2 * (cache + tok)
    mine = jnp.concatenate([own.reshape(rows, width), other.reshape(rows, width)], axis=0)
    line = lax.all_gather(mine, "y", axis=0, tiled=True)
    parts = lambda a: a.reshape(-1, nc, 2, 2, cache + tok, width)
    half = line.shape[0] // 2
    before = moved(line, sizes, dx=1)
    after = moved(line, sizes, dx=-1)
    state = stage(place, order, [q_own, q_other], [parts(line)], [(0, 0)], None, tok, cache)
    far_a = moved(before[:half], sizes, dx=1)
    far_b = moved(after[half:], sizes, dx=-1)
    state = stage(place, order, [q_own, q_other], [parts(before), parts(after)], [(nx - 1, 0), (1, 0)], state, tok, cache)
    final = [parts(far_a), parts(far_b)]
    spots = [(2, 0), (2, ny // 2)]
    result, theirs = stage(place, order, [q_own, q_other], final, spots, state, tok, cache, last=True)
    theirs = moved(theirs, sizes, dc=1)
    return put(place, theirs, result)[None]


def solution(mesh):
    nz, nctx, ntp = mesh.devices.shape
    nx = ny = 4
    nc = nctx // (nx * ny)
    fine = Mesh(mesh.devices.reshape(nz, nx, ny, nc, ntp), ("pipe", "x", "y", "core", "tp"))
    split = P("pipe", ("x", "y", "core"), "tp", None)
    return jax.shard_map(
        functools.partial(on_device, sizes=(nz, nx, ny, nc)),
        mesh=fine,
        in_specs=(split,) * 6 + (P("pipe", None),),
        out_specs=split,
        check_vma=False,
    )
```

time: 191 us -> 124 us (0.65)
  waiting for transfers between devices: 104 us -> 19.5 us
  Pallas kernels: 0 us -> 40.7 us
  matrix products: 39.9 us -> 0 us
  starting transfers between devices: 3.28 us -> 34.9 us
  other arithmetic: 26 us -> 0.09 us
  blocking collectives: 0 us -> 20.2 us
  between operations: 13.5 us -> 0.17 us
  local copies, waits for them, and re-layouts: 3.63 us -> 7.75 us
    all_gather x1 -> x0, waiting for transfers between devices: 78.2 us -> none  [on_device(): lax.all_gather(own_block, 'ctx', axis=0, tiled=True)]
    pallas_call x0 -> x5, Pallas kernels: none -> 40.7 us  [the longest x3 38.5 us: stage(): pl.pallas_call(body, grid_spec=pltpu.PrefetchScalarGridSpec(num_scalar_pr...]
    dot_general x2 -> x0, matrix products: 39.9 us -> none  [the longest x1 20.1 us: attend(): jnp.einsum('tgqd,kgd->gqtk', grouped, keys, preferred_element_type=jnp.fl...]
    ppermute x1 -> x10, starting transfers between devices: 3.28 us -> 34.9 us  [moved(): return lax.ppermute(value, FLAT, pairs)]
    reduce_sum x3 -> x0, other arithmetic: 23.4 us -> none  [the longest x1 21.7 us: attend(): total = total * rescale + jnp.sum(expo, axis=-1)]
    all_gather x0 -> x1, blocking collectives: none -> 20.2 us  [relay(): line = lax.all_gather(mine, 'y', axis=0, tiled=True)]
    ppermute x1 -> x10, waiting for transfers between devices: 25.6 us -> 19.5 us  [moved(): return lax.ppermute(value, FLAT, pairs)]
    dynamic_slice x0 -> x1, local copies, waits for them, and re-layouts: none -> 2.25 us  [relay(): lax.dynamic_slice_in_dim(queries[0], (1 - core) * half_heads, half_heads, 1)]
  transfers between devices with their start and end apart: 2 -> 10, of which waited for: 2 -> 6; matrix products, arithmetic and copies ran while one was open for 1% -> 3% of each run, Pallas kernels for 0% -> 17%
where the time goes in v1:
time: 124 us; the launch traced here: 123 us
  Pallas kernels  40.7 us (33%)
  starting transfers between devices  34.9 us (28%)
  blocking collectives  20.2 us (16%)
  waiting for transfers between devices  19.5 us (16%)
  local copies, waits for them, and re-layouts  7.75 us (6%)
    pallas_call x3, Pallas kernels, stage(): pl.pallas_call(body, grid_spec=pltpu.PrefetchScalarGridSpec(num_scalar_pr...  38.5 us
    ppermute x10, starting transfers between devices, moved(): return lax.ppermute(value, FLAT, pairs)  34.9 us
    all_gather x1, blocking collectives, relay(): line = lax.all_gather(mine, 'y', axis=0, tiled=True)  20.2 us
    ppermute x10, waiting for transfers between devices, moved(): return lax.ppermute(value, FLAT, pairs)  19.5 us
    unnamed x12, local copies, waits for them, and re-layouts  3.89 us
  transfers between devices with their start and end apart: 10, of which 6 were waited for; matrix products, arithmetic and copies ran while one was open for 3% of the time, Pallas kernels for 17%

profile of v1, /device:TPU:1, one launch (start us, length us, event | category | flops | bytes accessed | tf_op | source)
XLA Modules:
  0.0 123.3 jit_solution(8827282442775532238)
XLA Ops:
  0.0 0.0 copy-start.5
  0.0 0.0 copy-start
  0.0 0.9 copy-done
  0.9 0.0 copy-start.1
  0.9 0.8 copy-done.1
  1.7 0.0 copy-start.2
  1.7 0.8 copy-done.2
  2.5 0.0 copy-start.3
  2.5 0.8 copy-done.3
  3.2 0.0 copy-start.4
  3.2 0.7 copy-done.4
  3.9 0.9 pack_kv.1
  4.8 4.8 %collective-permute-start.3 = (bf16[2,2,96,128]{3,2,1,0:T(8,128)(2,1)S(1)}, bf16[2,2,96,128]{3,2,1,0:T(8,128)(2,1)S(1)}, u32[]{:S(2)}, u32[]{:S(2)}) collective-permute-start(bf16[2,2,96,128]{3,2,1,0:T(8,128)(2,1)S(1)} %get-tuple-element.13), channel_id=1, source_target_pairs={{0,64},{2,66},{4,68},{6,70},{8,72},{10,74},{12,76},{14,78},{16,80}... | collective-permute-start | bytes 294920 | tf_op jit(solution)/shard_map/ppermute | solution.py:30
  9.6 4.8 %collective-permute-start.4 = (bf16[2,2,96,128]{3,2,1,0:T(8,128)(2,1)S(1)}, bf16[2,2,96,128]{3,2,1,0:T(8,128)(2,1)S(1)}, u32[]{:S(2)}, u32[]{:S(2)}) collective-permute-start(bf16[2,2,96,128]{3,2,1,0:T(8,128)(2,1)S(1)} %get-tuple-element.14), channel_id=1, source_target_pairs={{0,66},{2,64},{4,70},{6,68},{8,74},{10,72},{12,78},{14,76},{16,82}... | collective-permute-start | bytes 294920 | tf_op jit(solution)/shard_map/ppermute | solution.py:30
  14.4 4.3 %collective-permute-done.3 = bf16[2,2,96,128]{3,2,1,0:T(8,128)(2,1)S(1)} collective-permute-done((bf16[2,2,96,128]{3,2,1,0:T(8,128)(2,1)S(1)}, bf16[2,2,96,128]{3,2,1,0:T(8,128)(2,1)S(1)}, u32[]{:S(2)}, u32[]{:S(2)}) %collective-permute-start.3) | collective-permute-done | bytes 98336 | tf_op jit(solution)/shard_map/ppermute | solution.py:30
  18.7 2.7 %collective-permute-done.4 = bf16[2,2,96,128]{3,2,1,0:T(8,128)(2,1)S(1)} collective-permute-done((bf16[2,2,96,128]{3,2,1,0:T(8,128)(2,1)S(1)}, bf16[2,2,96,128]{3,2,1,0:T(8,128)(2,1)S(1)}, u32[]{:S(2)}, u32[]{:S(2)}) %collective-permute-start.4) | collective-permute-done | bytes 98336 | tf_op jit(solution)/shard_map/ppermute | solution.py:30
  21.4 20.2 %all_gather.3 = bf16[3072,128]{1,0:T(8,128)(2,1)S(1)} all-gather(bf16[768,128]{1,0:T(8,128)(2,1)S(1)} %pad_maximum_fusion), channel_id=1, replica_groups=mesh['pipe'=8,'x'=4,'y'=4,'core'=2,'tp'=2] {'y'}, dimensions={0}, use_global_device_ids=true | all-gather | bytes 983040 | tf_op jit(solution)/shard_map/all_gather | solution.py:287
  41.6 3.1 %collective-permute-start.5 = (bf16[3072,128]{1,0:T(8,128)(2,1)S(1)}, bf16[3072,128]{1,0:T(8,128)(2,1)S(1)}, u32[]{:S(2)}, u32[]{:S(2)}) collective-permute-start(bf16[3072,128]{1,0:T(8,128)(2,1)S(1)} %all_gather.3), channel_id=1, source_target_pairs={{0,16},{2,18},{4,20},{6,22},{8,24},{10,26},{12,28},{14,30},{16,32}... | collective-permute-start | bytes 2359304 | tf_op jit(solution)/shard_map/ppermute | solution.py:30
  44.7 3.4 %collective-permute-start.7 = (bf16[3072,128]{1,0:T(8,128)(2,1)S(1)}, bf16[3072,128]{1,0:T(8,128)(2,1)S(1)}, u32[]{:S(2)}, u32[]{:S(2)}) collective-permute-start(bf16[3072,128]{1,0:T(8,128)(2,1)S(1)} %all_gather.3), channel_id=1, source_target_pairs={{0,48},{2,50},{4,52},{6,54},{8,56},{10,58},{12,60},{14,62},{16,0},... | collective-permute-start | bytes 2359304 | tf_op jit(solution)/shard_map/ppermute | solution.py:30
  48.1 2.3 %dynamic-slice_bitcast_fusion = (bf16[64,32,128]{2,1,0:T(8,128)(2,1)}, bf16[64,32,128]{2,1,0:T(8,128)(2,1)}) fusion(bf16[1,64,64,128]{3,2,1,0:T(8,128)(2,1)} %param.7, s32[]{:T(128)S(6)} %select_n.7, s32[]{:T(128)S(6)} %select_n.6), kind=kLoop, calls=%fused_computation | loop fusion | bytes 2097160 | tf_op jit(solution)/shard_map/dynamic_slice | solution.py:282
  50.3 1.9 %collective-permute-start.1 = (bf16[64,32,128]{2,1,0:T(8,128)(2,1)}, bf16[64,32,128]{2,1,0:T(8,128)(2,1)S(1)}, u32[]{:S(2)}, u32[]{:S(2)}) collective-permute-start(bf16[64,32,128]{2,1,0:T(8,128)(2,1)} %get-tuple-element.22), channel_id=1, source_target_pairs={{0,64},{2,66},{4,68},{6,70},{8,72},{10,74},{12,76},{14,78},{16,80}... | collective-permute-start | bytes 1572872 | tf_op jit(solution)/shard_map/ppermute | solution.py:30
  52.3 5.1 %collective-permute-start.2 = (bf16[64,32,128]{2,1,0:T(8,128)(2,1)}, bf16[64,32,128]{2,1,0:T(8,128)(2,1)S(1)}, u32[]{:S(2)}, u32[]{:S(2)}) collective-permute-start(bf16[64,32,128]{2,1,0:T(8,128)(2,1)} %get-tuple-element.21), channel_id=1, source_target_pairs={{0,66},{2,64},{4,70},{6,68},{8,74},{10,72},{12,78},{14,76},{16,82}... | collective-permute-start | bytes 1572872 | tf_op jit(solution)/shard_map/ppermute | solution.py:30
  57.4 4.9 %collective-permute-done.5 = bf16[3072,128]{1,0:T(8,128)(2,1)S(1)} collective-permute-done((bf16[3072,128]{1,0:T(8,128)(2,1)S(1)}, bf16[3072,128]{1,0:T(8,128)(2,1)S(1)}, u32[]{:S(2)}, u32[]{:S(2)}) %collective-permute-start.5) | collective-permute-done | bytes 786464 | tf_op jit(solution)/shard_map/ppermute | solution.py:30
  62.2 0.8 slice.8
  63.0 1.9 %collective-permute-start.6 = (bf16[1536,128]{1,0:T(8,128)(2,1)}, bf16[1536,128]{1,0:T(8,128)(2,1)}, u32[]{:S(2)}, u32[]{:S(2)}) collective-permute-start(bf16[1536,128]{1,0:T(8,128)(2,1)} %slice.8), channel_id=1, source_target_pairs={{0,16},{2,18},{4,20},{6,22},{8,24},{10,26},{12,28},{14,30},{16,32}... | collective-permute-start | bytes 1179656 | tf_op jit(solution)/shard_map/ppermute | solution.py:30
  64.9 0.0 collective-permute-done.7
  64.9 0.8 slice.9
  65.8 4.6 %collective-permute-start.8 = (bf16[1536,128]{1,0:T(8,128)(2,1)}, bf16[1536,128]{1,0:T(8,128)(2,1)}, u32[]{:S(2)}, u32[]{:S(2)}) collective-permute-start(bf16[1536,128]{1,0:T(8,128)(2,1)} %slice.9), channel_id=1, source_target_pairs={{0,48},{2,50},{4,52},{6,54},{8,56},{10,58},{12,60},{14,62},{16,0},... | collective-permute-start | bytes 1179656 | tf_op jit(solution)/shard_map/ppermute | solution.py:30
  70.3 0.0 copy-done.5
  70.3 1.9 %collective-permute-start = (s32[1,64]{1,0:T(1,128)S(1)}, s32[1,64]{1,0:T(1,128)S(1)}, u32[]{:S(2)}, u32[]{:S(2)}) collective-permute-start(s32[1,64]{1,0:T(1,128)S(1)} %copy-done.5), channel_id=1, source_target_pairs={{0,64},{2,66},{4,68},{6,70},{8,72},{10,74},{12,76},{14,78},{16,80}... | collective-permute-start | bytes 776 | tf_op jit(solution)/shard_map/ppermute | solution.py:30
  72.3 0.1 pad_add_fusion.refs_0_.place_ref
  72.4 4.0 %collective-permute-done.refs_1_ = s32[1,64]{1,0:T(1,128)S(1)} collective-permute-done((s32[1,64]{1,0:T(1,128)S(1)}, s32[1,64]{1,0:T(1,128)S(1)}, u32[]{:S(2)}, u32[]{:S(2)}) %collective-permute-start) | collective-permute-done | bytes 288 | tf_op jit(solution)/shard_map/ppermute | solution.py:30
  76.4 0.0 collective-permute-done.1.refs_2_
  76.4 2.2 %collective-permute-done.2.refs_3_ = bf16[64,32,128]{2,1,0:T(8,128)(2,1)S(1)} collective-permute-done((bf16[64,32,128]{2,1,0:T(8,128)(2,1)}, bf16[64,32,128]{2,1,0:T(8,128)(2,1)S(1)}, u32[]{:S(2)}, u32[]{:S(2)}) %collective-permute-start.2) | collective-permute-done | bytes 524320 | tf_op jit(solution)/shard_map/ppermute | solution.py:30
  78.5 7.2 %stage.2 = (f32[2,2048,256]{2,1,0:T(8,128)S(1)}, f32[2,2048,128]{2,1,0:T(8,128)S(1)}) custom-call(s32[5]{0:T(128)S(1)} %pad_add_fusion.refs_0_.place_ref, s32[1,64]{1,0:T(1,128)S(1)} %collective-permute-done.refs_1_, bf16[64,32,128]{2,1,0:T(8,128)(2,1)S(1)} %collective-permute-done.1.refs_2_, bf16[64,32,128]{2,1,0:T(8,128)(2,1)S(1)} %collective-permute-done.2.refs_3_, ...), custom_call_target="tpu_custom_call" | custom-call | tf_op jit(solution)/shard_map/stage/pallas_call | solution.py:229
  85.7 13.3 %stage.3 = (f32[2,2048,256]{2,1,0:T(8,128)S(1)}, f32[2,2048,128]{2,1,0:T(8,128)S(1)}) custom-call(s32[5]{0:T(128)S(1)} %pad_add_fusion.refs_0_.place_ref, s32[1,64]{1,0:T(1,128)S(1)} %collective-permute-done.refs_1_, bf16[64,32,128]{2,1,0:T(8,128)(2,1)S(1)} %collective-permute-done.1.refs_2_, bf16[64,32,128]{2,1,0:T(8,128)(2,1)S(1)} %collective-permute-done.2.refs_3_, ...), custom_call_target="tpu_custom_call" | custom-call | tf_op jit(solution)/shard_map/stage/pallas_call | solution.py:229
  99.0 0.0 collective-permute-done.6
  99.0 0.0 collective-permute-done.8
  99.0 18.0 %stage_last.1 = (bf16[64,64,128]{2,1,0:T(8,128)(2,1)}, bf16[64,32,128]{2,1,0:T(8,128)(2,1)S(1)}) custom-call(s32[5]{0:T(128)S(1)} %pad_add_fusion.refs_0_.place_ref, s32[1,64]{1,0:T(1,128)S(1)} %collective-permute-done.refs_1_, bf16[64,32,128]{2,1,0:T(8,128)(2,1)S(1)} %collective-permute-done.1.refs_2_, ...), custom_call_target="tpu_custom_call" | custom-call | tf_op jit(solution)/shard_map/stage_last/pallas_call | solution.py:229
  117.1 3.4 %collective-permute-start.9 = (bf16[64,32,128]{2,1,0:T(8,128)(2,1)S(1)}, bf16[64,32,128]{2,1,0:T(8,128)(2,1)S(1)}, u32[]{:S(2)}, u32[]{:S(2)}) collective-permute-start(bf16[64,32,128]{2,1,0:T(8,128)(2,1)S(1)} %get-tuple-element.19), channel_id=1, source_target_pairs={{0,2},{2,0},{4,6},{6,4},{8,10},{10,8},{12,14},{14,12},{16,18},{18,... | collective-permute-start | bytes 1572872 | tf_op jit(solution)/shard_map/ppermute | solution.py:30
  120.4 1.5 %collective-permute-done.9.part_ref = bf16[64,32,128]{2,1,0:T(8,128)(2,1)S(1)} collective-permute-done((bf16[64,32,128]{2,1,0:T(8,128)(2,1)S(1)}, bf16[64,32,128]{2,1,0:T(8,128)(2,1)S(1)}, u32[]{:S(2)}, u32[]{:S(2)}) %collective-permute-start.9) | collective-permute-done | bytes 524320 | tf_op jit(solution)/shard_map/ppermute | solution.py:30
  121.9 1.3 %put.1 = bf16[64,64,128]{2,1,0:T(8,128)(2,1)} custom-call(s32[5]{0:T(128)S(1)} %pad_add_fusion.refs_0_.place_ref, bf16[64,32,128]{2,1,0:T(8,128)(2,1)S(1)} %collective-permute-done.9.part_ref, bf16[64,64,128]{2,1,0:T(8,128)(2,1)} %get-tuple-element.20.whole_ref), custom_call_target="tpu_custom_call", output_to_operand_aliasing={{}: (2, {})} | custom-call | tf_op jit(solution)/shard_map/put/pallas_call | solution.py:253
  (2 shorter events, 0.0 us)
Async XLA Ops:
  0.0 70.3 %copy-start.5 = (s32[1,64]{1,0:T(1,128)S(1)}, s32[1,64]{1,0:T(1,128)}, u32[]{:S(2)}) copy-start(s32[1,64]{1,0:T(1,128)} %param.13) | copy-start | bytes 772
  0.0 0.9 copy-start
  0.9 0.8 copy-start.1
  1.7 0.8 copy-start.2
  2.5 0.8 copy-start.3
  3.2 0.7 copy-start.4
  4.8 14.0 %collective-permute-start.3 = (bf16[2,2,96,128]{3,2,1,0:T(8,128)(2,1)S(1)}, bf16[2,2,96,128]{3,2,1,0:T(8,128)(2,1)S(1)}, u32[]{:S(2)}, u32[]{:S(2)}) collective-permute-start(bf16[2,2,96,128]{3,2,1,0:T(8,128)(2,1)S(1)} %get-tuple-element.13), channel_id=1, source_target_pairs={{0,64},{2,66},{4,68},{6,70},{8,72},{10,74},{12,76},{14,78},{16,80}... | collective-permute-start | bytes 294920 | tf_op jit(solution)/shard_map/ppermute | solution.py:30
  9.6 11.8 %collective-permute-start.4 = (bf16[2,2,96,128]{3,2,1,0:T(8,128)(2,1)S(1)}, bf16[2,2,96,128]{3,2,1,0:T(8,128)(2,1)S(1)}, u32[]{:S(2)}, u32[]{:S(2)}) collective-permute-start(bf16[2,2,96,128]{3,2,1,0:T(8,128)(2,1)S(1)} %get-tuple-element.14), channel_id=1, source_target_pairs={{0,66},{2,64},{4,70},{6,68},{8,74},{10,72},{12,78},{14,76},{16,82}... | collective-permute-start | bytes 294920 | tf_op jit(solution)/shard_map/ppermute | solution.py:30
  41.6 20.6 %collective-permute-start.5 = (bf16[3072,128]{1,0:T(8,128)(2,1)S(1)}, bf16[3072,128]{1,0:T(8,128)(2,1)S(1)}, u32[]{:S(2)}, u32[]{:S(2)}) collective-permute-start(bf16[3072,128]{1,0:T(8,128)(2,1)S(1)} %all_gather.3), channel_id=1, source_target_pairs={{0,16},{2,18},{4,20},{6,22},{8,24},{10,26},{12,28},{14,30},{16,32}... | collective-permute-start | bytes 2359304 | tf_op jit(solution)/shard_map/ppermute | solution.py:30
  44.7 20.2 %collective-permute-start.7 = (bf16[3072,128]{1,0:T(8,128)(2,1)S(1)}, bf16[3072,128]{1,0:T(8,128)(2,1)S(1)}, u32[]{:S(2)}, u32[]{:S(2)}) collective-permute-start(bf16[3072,128]{1,0:T(8,128)(2,1)S(1)} %all_gather.3), channel_id=1, source_target_pairs={{0,48},{2,50},{4,52},{6,54},{8,56},{10,58},{12,60},{14,62},{16,0},... | collective-permute-start | bytes 2359304 | tf_op jit(solution)/shard_map/ppermute | solution.py:30
  50.3 26.0 %collective-permute-start.1 = (bf16[64,32,128]{2,1,0:T(8,128)(2,1)}, bf16[64,32,128]{2,1,0:T(8,128)(2,1)S(1)}, u32[]{:S(2)}, u32[]{:S(2)}) collective-permute-start(bf16[64,32,128]{2,1,0:T(8,128)(2,1)} %get-tuple-element.22), channel_id=1, source_target_pairs={{0,64},{2,66},{4,68},{6,70},{8,72},{10,74},{12,76},{14,78},{16,80}... | collective-permute-start | bytes 1572872 | tf_op jit(solution)/shard_map/ppermute | solution.py:30
  52.3 26.3 %collective-permute-start.2 = (bf16[64,32,128]{2,1,0:T(8,128)(2,1)}, bf16[64,32,128]{2,1,0:T(8,128)(2,1)S(1)}, u32[]{:S(2)}, u32[]{:S(2)}) collective-permute-start(bf16[64,32,128]{2,1,0:T(8,128)(2,1)} %get-tuple-element.21), channel_id=1, source_target_pairs={{0,66},{2,64},{4,70},{6,68},{8,74},{10,72},{12,78},{14,76},{16,82}... | collective-permute-start | bytes 1572872 | tf_op jit(solution)/shard_map/ppermute | solution.py:30
  63.0 36.0 %collective-permute-start.6 = (bf16[1536,128]{1,0:T(8,128)(2,1)}, bf16[1536,128]{1,0:T(8,128)(2,1)}, u32[]{:S(2)}, u32[]{:S(2)}) collective-permute-start(bf16[1536,128]{1,0:T(8,128)(2,1)} %slice.8), channel_id=1, source_target_pairs={{0,16},{2,18},{4,20},{6,22},{8,24},{10,26},{12,28},{14,30},{16,32}... | collective-permute-start | bytes 1179656 | tf_op jit(solution)/shard_map/ppermute | solution.py:30
  65.8 33.3 %collective-permute-start.8 = (bf16[1536,128]{1,0:T(8,128)(2,1)}, bf16[1536,128]{1,0:T(8,128)(2,1)}, u32[]{:S(2)}, u32[]{:S(2)}) collective-permute-start(bf16[1536,128]{1,0:T(8,128)(2,1)} %slice.9), channel_id=1, source_target_pairs={{0,48},{2,50},{4,52},{6,54},{8,56},{10,58},{12,60},{14,62},{16,0},... | collective-permute-start | bytes 1179656 | tf_op jit(solution)/shard_map/ppermute | solution.py:30
  70.3 6.0 %collective-permute-start = (s32[1,64]{1,0:T(1,128)S(1)}, s32[1,64]{1,0:T(1,128)S(1)}, u32[]{:S(2)}, u32[]{:S(2)}) collective-permute-start(s32[1,64]{1,0:T(1,128)S(1)} %copy-done.5), channel_id=1, source_target_pairs={{0,64},{2,66},{4,68},{6,70},{8,72},{10,74},{12,76},{14,78},{16,80}... | collective-permute-start | bytes 776 | tf_op jit(solution)/shard_map/ppermute | solution.py:30
  117.1 4.9 %collective-permute-start.9 = (bf16[64,32,128]{2,1,0:T(8,128)(2,1)S(1)}, bf16[64,32,128]{2,1,0:T(8,128)(2,1)S(1)}, u32[]{:S(2)}, u32[]{:S(2)}) collective-permute-start(bf16[64,32,128]{2,1,0:T(8,128)(2,1)S(1)} %get-tuple-element.19), channel_id=1, source_target_pairs={{0,2},{2,0},{4,6},{6,4},{8,10},{10,8},{12,14},{14,12},{16,18},{18,... | collective-permute-start | bytes 1572872 | tf_op jit(solution)/shard_map/ppermute | solution.py:30

commit v2 on v1

--- a/solution.py
+++ b/solution.py
@@ -45,7 +45,7 @@
     return jnp.where(hit, scale(token // CBLK, head), 0.0).astype(jnp.bfloat16)
 
 
-def pack_body(core_ref, exps_ref, sk_ref, sv_ref, ck_ref, cv_ref, own_ref, other_ref, *, heads):
+def pack_body(core_ref, exps_ref, order_ref, sk_ref, sv_ref, ck_ref, cv_ref, own_ref, other_ref, *, heads):
     core = core_ref[0]
     tok = sk_ref.shape[0] // heads
     cache = ck_ref.shape[0] // heads
@@ -66,25 +66,28 @@
             moved_span = jnp.dot(span_pick, span[...], preferred_element_type=jnp.float32).astype(jnp.bfloat16)
             moved_cache = jnp.dot(cache_pick, cached[...], preferred_element_type=jnp.float32).astype(jnp.bfloat16)
             for h in range(2):
-                ref[h, kv, :cache] = moved_cache[h * cache : (h + 1) * cache]
-                ref[h, kv, cache:] = moved_span[h * tok : (h + 1) * tok]
-
-
-def pack(core, exps, span_keys, span_values, cache_keys, cache_values):
+                at = (2 * h + kv) * (cache + tok)
+                ref[at : at + cache] = moved_cache[h * cache : (h + 1) * cache]
+                ref[at + cache : at + cache + tok] = moved_span[h * tok : (h + 1) * tok]
+    order = order_ref[...].astype(jnp.float32)
+    order = jnp.concatenate([order, jnp.zeros((1, HD - order.shape[1]), jnp.float32)], axis=1)
+    own_ref[4 * (cache + tok) :] = jnp.broadcast_to(order, (16, HD)).astype(jnp.bfloat16)
+
+
+def pack(core, exps, order, span_keys, span_values, cache_keys, cache_values):
     tok, heads, width = span_keys.shape
     cache = cache_keys.shape[0]
     flat = lambda a: a.reshape(-1, width)
-    shape = jax.ShapeDtypeStruct((2, 2, cache + tok, width), jnp.bfloat16)
+    rows = 4 * (cache + tok)
     smem = pl.BlockSpec(memory_space=pltpu.SMEM)
     vmem = pl.BlockSpec(memory_space=pltpu.VMEM)
     return pl.pallas_call(
         functools.partial(pack_body, heads=heads),
-        out_shape=(shape, shape),
-        in_specs=[smem, smem, vmem, vmem, vmem, vmem],
+        out_shape=(jax.ShapeDtypeStruct((rows + 16, width), jnp.bfloat16), jax.ShapeDtypeStruct((rows, width), jnp.bfloat16)),
+        in_specs=[smem, smem, vmem, vmem, vmem, vmem, vmem],
         out_specs=(vmem, vmem),
-        compiler_params=pltpu.CompilerParams(vmem_limit_bytes=8 << 20),
         name="pack_kv",
-    )(core, exps, flat(span_keys), flat(span_values), flat(cache_keys), flat(cache_values))
+    )(core, exps, order, flat(span_keys), flat(span_values), flat(cache_keys), flat(cache_values))
 
 
 def fill(place_ref, order_ref, chunk_refs, spots, ka, va, head_slot, tok, cache):
@@ -119,10 +122,10 @@
     va[:, HD:] = jnp.ones((va.shape[0], HD), jnp.bfloat16)
 
 
-def stage_body(*refs, nq, nchunk, spots, first, last, tok, cache, tile_tok, sub):
+def stage_body(*refs, nchunk, spots, first, last, tok, cache, sub, ahead, lag):
     place_ref, order_ref = refs[0], refs[1]
     refs = refs[2:]
-    q_refs, refs = refs[:nq], refs[nq:]
+    q_refs, refs = refs[:2], refs[2:]
     chunk_refs, refs = refs[:nchunk], refs[nchunk:]
     if not first:
         (acc_in, max_in), refs = refs[:2], refs[2:]
@@ -131,14 +134,7 @@
     else:
         (acc_out, max_out), refs = refs[:2], refs[2:]
     ka, va = refs
-    head = pl.program_id(0)
-    tile = pl.program_id(1)
-
-    @pl.when(tile == 0)
-    def _():
-        fill(place_ref, order_ref, chunk_refs, spots, ka, va, head, tok, cache)
-
-    rows = tile_tok * GROUP
+    fill(place_ref, order_ref, chunk_refs, spots, ka, va, pl.program_id(0), tok, cache)
     factor = math.log2(math.e) / math.sqrt(HD)
     if last:
         i, j = iota((HD, HD), 0), iota((HD, HD), 1)
@@ -148,19 +144,36 @@
         bits = (bits ^ (bits >> 1)) & 1
         signs = (1.0 - 2.0 * bits.astype(jnp.float32)).astype(jnp.bfloat16)
         signs = jnp.concatenate([signs, signs], axis=0)
-    for s in range(rows // sub):
-        tok0 = s * sub // GROUP
-        tok1 = (s + 1) * sub // GROUP
-        part = q_refs[0][tok0:tok1].reshape(sub, HD)
-        if nq == 2:
-            other = q_refs[1][tok0:tok1].reshape(sub, HD)
-            part = jnp.where(tile < tok // tile_tok, part, other)
-        token = tile * tile_tok + tok0 + iota((sub, HD), 0) // GROUP
+    toks = sub // GROUP
+    pieces = 2 * tok // toks
+
+    def scores(s):
+        tok0 = s * toks
+        ref = q_refs[tok0 // tok]
+        part = ref[tok0 % tok : tok0 % tok + toks].reshape(sub, HD)
+        token = tok0 + iota((sub, HD), 0) // GROUP
         hot = jnp.where(iota((sub, HD), 1) == token, 1.0, 0.0).astype(jnp.bfloat16)
         left = jnp.concatenate([part, hot], axis=1)
-        score = lax.dot_general(left, ka[...], (((1,), (1,)), ((), ())), preferred_element_type=jnp.float32)
+        return lax.dot_general(left, ka[...], (((1,), (1,)), ((), ())), preferred_element_type=jnp.float32)
+
+    def finish(s, acc):
+        mixed = acc[:, :HD] * (1.0 / (acc[:, HD:] * math.sqrt(HD)))
+        high = mixed.astype(jnp.bfloat16)
+        low = (mixed - high.astype(jnp.float32)).astype(jnp.bfloat16)
+        turned = jnp.dot(jnp.concatenate([high, low], axis=1), signs, preferred_element_type=jnp.float32)
+        turned = turned.astype(jnp.bfloat16).reshape(toks, GROUP, HD)
+        ref = (own_ref, other_ref)[s * toks // tok]
+        ref[s * toks % tok : s * toks % tok + toks] = turned
+
+    ready = [scores(s) for s in range(ahead)]
+    waiting = []
+    for s in range(pieces):
+        if s + ahead < pieces:
+            ready.append(scores(s + ahead))
+        score = ready[s]
+        ready[s] = None
+        span = slice(s * sub, (s + 1) * sub)
         top = jnp.max(score, axis=1, keepdims=True)
-        span = slice(s * sub, (s + 1) * sub)
         if not first:
             top_old = max_in[0, span, :1]
             top = jnp.maximum(top, top_old)
@@ -169,48 +182,35 @@
         if not first:
             acc = acc + acc_in[0, span] * jnp.exp2((top_old - top) * factor)
         if last:
-            mixed = acc[:, :HD] / (acc[:, HD:] * math.sqrt(HD))
-            high = mixed.astype(jnp.bfloat16)
-            low = (mixed - high.astype(jnp.float32)).astype(jnp.bfloat16)
-            turned = jnp.dot(jnp.concatenate([high, low], axis=1), signs, preferred_element_type=jnp.float32)
-            turned = turned.astype(jnp.bfloat16).reshape(sub // GROUP, GROUP, HD)
-
-            @pl.when(tile < tok // tile_tok)
-            def _():
-                own_ref[tok0:tok1] = turned
-
-            @pl.when(tile >= tok // tile_tok)
-            def _():
-                other_ref[tok0:tok1] = turned
+            waiting.append((s, acc))
+            if len(waiting) > lag:
+                finish(*waiting.pop(0))
         else:
             acc_out[0, span] = acc
             max_out[0, span] = jnp.broadcast_to(top, (sub, HD))
-
-
-def stage(place, order, queries, chunks, spots, state, tok, cache, last=False, tile_tok=64, sub=256):
-    nq = len(queries)
-    per = queries[0].shape[0] // tile_tok
-    tiles = nq * per
-    rows = tile_tok * GROUP
+    for item in waiting:
+        finish(*item)
+
+
+def stage(place, order, queries, chunks, spots, state, tok, cache, last=False, sub=512, ahead=1, lag=1):
     total = 2 * tok * GROUP
     keys = sum(c.shape[0] for c in chunks) * 2 * (cache + tok)
-    smem = pl.BlockSpec(memory_space=pltpu.SMEM)
     first = state is None
-    in_specs = [smem]
-    for n in range(nq):
-        in_specs.append(pl.BlockSpec((tile_tok, GROUP, HD), lambda h, t, p, n=n: (jnp.clip(t - n * per, 0, per - 1), h, 0)))
+    in_specs = [pl.BlockSpec(memory_space=pltpu.SMEM)]
+    for _ in queries:
+        in_specs.append(pl.BlockSpec((tok, GROUP, HD), lambda h, p: (0, 2 * p[2] + h, 0)))
     for c in chunks:
-        in_specs.append(pl.BlockSpec(c.shape, lambda h, t, p, nd=c.ndim: (0,) * nd, pipeline_mode=pl.Buffered(1)))
-    acc_spec = pl.BlockSpec((1, rows, 2 * HD), lambda h, t, p: (h, t, 0))
-    max_spec = pl.BlockSpec((1, rows, HD), lambda h, t, p: (h, t, 0))
+        in_specs.append(pl.BlockSpec(c.shape, lambda h, p, nd=c.ndim: (0,) * nd, pipeline_mode=pl.Buffered(1)))
+    acc_spec = pl.BlockSpec((1, total, 2 * HD), lambda h, p: (h, 0, 0))
+    max_spec = pl.BlockSpec((1, total, HD), lambda h, p: (h, 0, 0))
     operands = [order, *queries, *chunks]
     if not first:
         in_specs += [acc_spec, max_spec]
         operands += list(state)
     if last:
         out_specs = (
-            pl.BlockSpec((tile_tok, GROUP, HD), lambda h, t, p: (jnp.minimum(t, per - 1), 2 * p[2] + h, 0)),
-            pl.BlockSpec((tile_tok, GROUP, HD), lambda h, t, p: (jnp.maximum(t - per, 0), h, 0)),
+            pl.BlockSpec((tok, GROUP, HD), lambda h, p: (0, 2 * p[2] + h, 0)),
+            pl.BlockSpec((tok, GROUP, HD), lambda h, p: (0, h, 0)),
         )
         out_shape = (
             jax.ShapeDtypeStruct((tok, 4 * GROUP, HD), jnp.bfloat16),
@@ -223,20 +223,19 @@
             jax.ShapeDtypeStruct((2, total, HD), jnp.float32),
         )
     body = functools.partial(
-        stage_body, nq=nq, nchunk=len(chunks), spots=spots, first=first, last=last, tok=tok, cache=cache,
-        tile_tok=tile_tok, sub=sub,
+        stage_body, nchunk=len(chunks), spots=spots, first=first, last=last, tok=tok, cache=cache, sub=sub, ahead=ahead, lag=lag
     )
     return pl.pallas_call(
         body,
         grid_spec=pltpu.PrefetchScalarGridSpec(
             num_scalar_prefetch=1,
-            grid=(2, tiles),
+            grid=(2,),
             in_specs=in_specs,
             out_specs=out_specs,
             scratch_shapes=[pltpu.VMEM((keys, 2 * HD), jnp.bfloat16), pltpu.VMEM((keys, 2 * HD), jnp.bfloat16)],
         ),
         out_shape=out_shape,
-        compiler_params=pltpu.CompilerParams(vmem_limit_bytes=32 << 20),
+        compiler_params=pltpu.CompilerParams(vmem_limit_bytes=36 << 20),
         name="stage_last" if last else "stage",
     )(place, *operands)
 
@@ -268,22 +267,19 @@
 
 def relay(queries, span_keys, span_values, cache_keys, cache_values, scale_exps, block_order, sizes):
     _, nx, ny, nc = sizes
-    tok, heads, width = queries.shape[1:]
+    tok, _, width = queries.shape[1:]
     cache = cache_keys.shape[1]
     core = lax.axis_index("core").astype(jnp.int32)
     place = jnp.stack([lax.axis_index("x").astype(jnp.int32), lax.axis_index("y").astype(jnp.int32), core, jnp.int32(nx), jnp.int32(ny)])
     exps = scale_exps[0].transpose(0, 2, 1)
-    own, other = pack(core.reshape(1), exps, span_keys[0], span_values[0], cache_keys[0], cache_values[0])
+    own, other = pack(core.reshape(1), exps, block_order, span_keys[0], span_values[0], cache_keys[0], cache_values[0])
     own = moved(own, sizes, dz=1)
     other = moved(other, sizes, dz=1, dc=1)
-    order = moved(block_order, sizes, dz=1)
-    half_heads = heads // 2
-    q_own = lax.dynamic_slice_in_dim(queries[0], core * half_heads, half_heads, 1)
-    q_other = lax.dynamic_slice_in_dim(queries[0], (1 - core) * half_heads, half_heads, 1)
-    q_own = moved(q_own, sizes, dz=1)
-    q_other = moved(q_other, sizes, dz=1, dc=1)
-    rows = 2 * 2 * (cache + tok)
-    mine = jnp.concatenate([own.reshape(rows, width), other.reshape(rows, width)], axis=0)
+    rows = 4 * (cache + tok)
+    order = own[rows : rows + 1, : block_order.shape[1]].astype(jnp.int32)
+    q_own = moved(queries[0], sizes, dz=1)
+    q_other = moved(q_own, sizes, dc=1)
+    mine = jnp.concatenate([own[:rows], other], axis=0)
     line = lax.all_gather(mine, "y", axis=0, tiled=True)
     parts = lambda a: a.reshape(-1, nc, 2, 2, cache + tok, width)
     half = line.shape[0] // 2
@@ -295,7 +291,7 @@
     state = stage(place, order, [q_own, q_other], [parts(before), parts(after)], [(nx - 1, 0), (1, 0)], state, tok, cache)
     final = [parts(far_a), parts(far_b)]
     spots = [(2, 0), (2, ny // 2)]
-    result, theirs = stage(place, order, [q_own, q_other], final, spots, state, tok, cache, last=True)
+    result, theirs = stage(place, order, [q_own, q_other], final, spots, state, tok, cache, last=True, ahead=2)
     theirs = moved(theirs, sizes, dc=1)
     return put(place, theirs, result)[None]
 

time: 124 us -> 125 us (level)
  waiting for transfers between devices: 19.5 us -> 36.4 us
  Pallas kernels: 40.7 us -> 28 us
  local copies, waits for them, and re-layouts: 7.75 us -> 4.16 us
    ppermute x10 -> x9, waiting for transfers between devices: 19.5 us -> 36.4 us  [moved(): return lax.ppermute(value, FLAT, pairs)]
    pallas_call x3, Pallas kernels: 38.5 us -> 24.8 us  [stage(): pl.pallas_call(body, grid_spec=pltpu.PrefetchScalarGridSpec(num_scalar_pr...]
    dynamic_slice x1 -> x0, local copies, waits for them, and re-layouts: 2.25 us -> none  [relay(): lax.dynamic_slice_in_dim(queries[0], (1 - core) * half_heads, half_heads, 1)]
    unnamed x12 -> x8, local copies, waits for them, and re-layouts: 3.89 us -> 2.46 us
    ppermute x10 -> x9, starting transfers between devices: 34.9 us -> 34.5 us  [moved(): return lax.ppermute(value, FLAT, pairs)]
  transfers between devices with their start and end apart: 10 -> 9, of which waited for: 6 -> 4; matrix products, arithmetic and copies ran while one was open for 3% -> 1% of each run, Pallas kernels for 17% -> 15%
where the time goes in v2:
time: 125 us; the launch traced here: 124 us
  waiting for transfers between devices  36.4 us (29%)
  starting transfers between devices  34.5 us (28%)
  Pallas kernels  28 us (22%)
  blocking collectives  20.9 us (17%)
  local copies, waits for them, and re-layouts  4.16 us (3%)
    ppermute x9, waiting for transfers between devices, moved(): return lax.ppermute(value, FLAT, pairs)  36.4 us
    ppermute x9, starting transfers between devices, moved(): return lax.ppermute(value, FLAT, pairs)  34.5 us
    pallas_call x3, Pallas kernels, stage(): pl.pallas_call(body, grid_spec=pltpu.PrefetchScalarGridSpec(num_scalar_pr...  24.8 us
    all_gather x1, blocking collectives, relay(): line = lax.all_gather(mine, 'y', axis=0, tiled=True)  20.9 us
  transfers between devices with their start and end apart: 9, of which 4 were waited for; matrix products, arithmetic and copies ran while one was open for 1% of the time, Pallas kernels for 15%

profile of v2, /device:TPU:1, one launch (start us, length us, event | category | flops | bytes accessed | tf_op | source)
XLA Modules:
  0.0 124.3 jit_solution(753032805283298833)
XLA Ops:
  0.0 4.8 %collective-permute-start.1 = (bf16[64,64,128]{2,1,0:T(8,128)(2,1)}, bf16[64,64,128]{2,1,0:T(8,128)(2,1)S(1)}, u32[]{:S(2)}, u32[]{:S(2)}) collective-permute-start(bf16[64,64,128]{2,1,0:T(8,128)(2,1)} %bitcast.26), channel_id=1, source_target_pairs={{0,64},{2,66},{4,68},{6,70},{8,72},{10,74},{12,76},{14,78},{16,80}... | collective-permute-start | bytes 3145736 | tf_op jit(solution)/shard_map/ppermute | solution.py:30
  4.8 1.9 %pack_kv.1 = (bf16[400,128]{1,0:T(8,128)(2,1)}, bf16[384,128]{1,0:T(8,128)(2,1)}) custom-call(s32[1]{0:T(128)} %bitcast.2.core_ref, s32[2,2,4]{2,1,0:T(2,128)} %bitcast.25, s32[1,64]{1,0:T(1,128)} %order_ref.1, bf16[256,128]{1,0:T(8,128)(2,1)} %bitcast.21, bf16[256,128]{1,0:T(8,128)(2,1)} %bitcast.22, bf16[128,128]{1,0:T(8,128)(2,1)} %bitcast.23, ...), custom_call_target="tpu_custom_call" | custom-call | tf_op jit(solution)/shard_map/pack_kv/pallas_call | solution.py:84
  6.7 4.0 %collective-permute-start = (bf16[400,128]{1,0:T(8,128)(2,1)}, bf16[400,128]{1,0:T(8,128)(2,1)S(1)}, u32[]{:S(2)}, u32[]{:S(2)}) collective-permute-start(bf16[400,128]{1,0:T(8,128)(2,1)} %get-tuple-element.13), channel_id=1, source_target_pairs={{0,64},{2,66},{4,68},{6,70},{8,72},{10,74},{12,76},{14,78},{16,80}... | collective-permute-start | bytes 307208 | tf_op jit(solution)/shard_map/ppermute | solution.py:30
  10.7 5.1 %collective-permute-start.3 = (bf16[384,128]{1,0:T(8,128)(2,1)}, bf16[384,128]{1,0:T(8,128)(2,1)S(1)}, u32[]{:S(2)}, u32[]{:S(2)}) collective-permute-start(bf16[384,128]{1,0:T(8,128)(2,1)} %get-tuple-element.14), channel_id=1, source_target_pairs={{0,66},{2,64},{4,70},{6,68},{8,74},{10,72},{12,78},{14,76},{16,82}... | collective-permute-start | bytes 294920 | tf_op jit(solution)/shard_map/ppermute | solution.py:30
  15.8 20.9 %collective-permute-done = bf16[400,128]{1,0:T(8,128)(2,1)S(1)} collective-permute-done((bf16[400,128]{1,0:T(8,128)(2,1)}, bf16[400,128]{1,0:T(8,128)(2,1)S(1)}, u32[]{:S(2)}, u32[]{:S(2)}) %collective-permute-start) | collective-permute-done | bytes 102432 | tf_op jit(solution)/shard_map/ppermute | solution.py:30
  36.7 2.7 %collective-permute-done.3 = bf16[384,128]{1,0:T(8,128)(2,1)S(1)} collective-permute-done((bf16[384,128]{1,0:T(8,128)(2,1)}, bf16[384,128]{1,0:T(8,128)(2,1)S(1)}, u32[]{:S(2)}, u32[]{:S(2)}) %collective-permute-start.3) | collective-permute-done | bytes 98336 | tf_op jit(solution)/shard_map/ppermute | solution.py:30
  39.4 20.9 %all_gather.3 = bf16[3072,128]{1,0:T(8,128)(2,1)S(1)} all-gather(bf16[768,128]{1,0:T(8,128)(2,1)S(1)} %pad_maximum_fusion), channel_id=1, replica_groups=mesh['pipe'=8,'x'=4,'y'=4,'core'=2,'tp'=2] {'y'}, dimensions={0}, use_global_device_ids=true | all-gather | bytes 983040 | tf_op jit(solution)/shard_map/all_gather | solution.py:283
  60.3 3.1 %collective-permute-start.4 = (bf16[3072,128]{1,0:T(8,128)(2,1)S(1)}, bf16[3072,128]{1,0:T(8,128)(2,1)S(1)}, u32[]{:S(2)}, u32[]{:S(2)}) collective-permute-start(bf16[3072,128]{1,0:T(8,128)(2,1)S(1)} %all_gather.3), channel_id=1, source_target_pairs={{0,16},{2,18},{4,20},{6,22},{8,24},{10,26},{12,28},{14,30},{16,32}... | collective-permute-start | bytes 2359304 | tf_op jit(solution)/shard_map/ppermute | solution.py:30
  63.5 3.4 %collective-permute-start.6 = (bf16[3072,128]{1,0:T(8,128)(2,1)S(1)}, bf16[3072,128]{1,0:T(8,128)(2,1)S(1)}, u32[]{:S(2)}, u32[]{:S(2)}) collective-permute-start(bf16[3072,128]{1,0:T(8,128)(2,1)S(1)} %all_gather.3), channel_id=1, source_target_pairs={{0,48},{2,50},{4,52},{6,54},{8,56},{10,58},{12,60},{14,62},{16,0},... | collective-permute-start | bytes 2359304 | tf_op jit(solution)/shard_map/ppermute | solution.py:30
  66.8 0.0 collective-permute-done.1.refs_2_
  66.9 3.4 %collective-permute-start.2 = (bf16[64,64,128]{2,1,0:T(8,128)(2,1)S(1)}, bf16[64,64,128]{2,1,0:T(8,128)(2,1)S(1)}, u32[]{:S(2)}, u32[]{:S(2)}) collective-permute-start(bf16[64,64,128]{2,1,0:T(8,128)(2,1)S(1)} %collective-permute-done.1.refs_2_), channel_id=1, source_target_pairs={{0,2},{2,0},{4,6},{6,4},{8,10},{10,8},{12,14},{14,12},{16,18},{18,... | collective-permute-start | bytes 3145736 | tf_op jit(solution)/shard_map/ppermute | solution.py:30
  70.3 11.3 %collective-permute-done.4 = bf16[3072,128]{1,0:T(8,128)(2,1)S(1)} collective-permute-done((bf16[3072,128]{1,0:T(8,128)(2,1)S(1)}, bf16[3072,128]{1,0:T(8,128)(2,1)S(1)}, u32[]{:S(2)}, u32[]{:S(2)}) %collective-permute-start.4) | collective-permute-done | bytes 786464 | tf_op jit(solution)/shard_map/ppermute | solution.py:30
  81.6 0.0 copy-start
  81.6 0.8 slice.18
  82.4 1.9 %collective-permute-start.5 = (bf16[1536,128]{1,0:T(8,128)(2,1)}, bf16[1536,128]{1,0:T(8,128)(2,1)S(1)}, u32[]{:S(2)}, u32[]{:S(2)}) collective-permute-start(bf16[1536,128]{1,0:T(8,128)(2,1)} %slice.18), channel_id=1, source_target_pairs={{0,16},{2,18},{4,20},{6,22},{8,24},{10,26},{12,28},{14,30},{16,32}... | collective-permute-start | bytes 1179656 | tf_op jit(solution)/shard_map/ppermute | solution.py:30
  84.4 0.0 collective-permute-done.6
  84.4 0.0 copy-done
  84.4 0.0 copy-start.2
  84.4 0.8 slice.19
  85.2 0.2 copy-done.2
  85.4 4.6 %collective-permute-start.7 = (bf16[1536,128]{1,0:T(8,128)(2,1)}, bf16[1536,128]{1,0:T(8,128)(2,1)}, u32[]{:S(2)}, u32[]{:S(2)}) collective-permute-start(bf16[1536,128]{1,0:T(8,128)(2,1)} %slice.19), channel_id=1, source_target_pairs={{0,48},{2,50},{4,52},{6,54},{8,56},{10,58},{12,60},{14,62},{16,0},... | collective-permute-start | bytes 1179656 | tf_op jit(solution)/shard_map/ppermute | solution.py:30
  90.0 0.1 pad_add_fusion.refs_0_.place_ref
  90.1 0.0 collective-permute-done.2.refs_3_
  90.1 6.0 %stage.2 = (f32[2,2048,256]{2,1,0:T(8,128)S(1)}, f32[2,2048,128]{2,1,0:T(8,128)S(1)}) custom-call(s32[5]{0:T(128)S(1)} %pad_add_fusion.refs_0_.place_ref, s32[1,64]{1,0:T(1,128)S(1)} %slice_convert_fusion.refs_1_, bf16[64,64,128]{2,1,0:T(8,128)(2,1)S(1)} %collective-permute-done.1.refs_2_, bf16[64,64,128]{2,1,0:T(8,128)(2,1)S(1)} %collective-permute-done.2.refs_3_, ...), custom_call_target="tpu_custom_call" | custom-call | tf_op jit(solution)/shard_map/stage/pallas_call | solution.py:228
  96.1 0.0 copy-start.1
  96.1 1.1 copy-done.1
  97.2 0.0 copy-start.3
  97.2 1.1 copy-done.3
  98.4 10.3 %stage.3 = (f32[2,2048,256]{2,1,0:T(8,128)S(1)}, f32[2,2048,128]{2,1,0:T(8,128)S(1)}) custom-call(s32[5]{0:T(128)S(1)} %pad_add_fusion.refs_0_.place_ref, s32[1,64]{1,0:T(1,128)S(1)} %slice_convert_fusion.refs_1_, bf16[64,64,128]{2,1,0:T(8,128)(2,1)S(1)} %collective-permute-done.1.refs_2_, bf16[64,64,128]{2,1,0:T(8,128)(2,1)S(1)} %collective-permute-done.2.refs_3_, ...), custom_call_target="tpu_custom_call" | custom-call | tf_op jit(solution)/shard_map/stage/pallas_call | solution.py:228
  108.7 0.0 collective-permute-done.5
  108.7 0.0 collective-permute-done.7
  108.7 8.5 %stage_last.1 = (bf16[64,64,128]{2,1,0:T(8,128)(2,1)}, bf16[64,32,128]{2,1,0:T(8,128)(2,1)S(1)}) custom-call(s32[5]{0:T(128)S(1)} %pad_add_fusion.refs_0_.place_ref, s32[1,64]{1,0:T(1,128)S(1)} %slice_convert_fusion.refs_1_, bf16[64,64,128]{2,1,0:T(8,128)(2,1)S(1)} %collective-permute-done.1.refs_2_, ...), custom_call_target="tpu_custom_call" | custom-call | tf_op jit(solution)/shard_map/stage_last/pallas_call | solution.py:228
  117.2 4.2 %collective-permute-start.8 = (bf16[64,32,128]{2,1,0:T(8,128)(2,1)S(1)}, bf16[64,32,128]{2,1,0:T(8,128)(2,1)S(1)}, u32[]{:S(2)}, u32[]{:S(2)}) collective-permute-start(bf16[64,32,128]{2,1,0:T(8,128)(2,1)S(1)} %get-tuple-element.19), channel_id=1, source_target_pairs={{0,2},{2,0},{4,6},{6,4},{8,10},{10,8},{12,14},{14,12},{16,18},{18,... | collective-permute-start | bytes 1572872 | tf_op jit(solution)/shard_map/ppermute | solution.py:30
  121.4 1.5 %collective-permute-done.8.part_ref = bf16[64,32,128]{2,1,0:T(8,128)(2,1)S(1)} collective-permute-done((bf16[64,32,128]{2,1,0:T(8,128)(2,1)S(1)}, bf16[64,32,128]{2,1,0:T(8,128)(2,1)S(1)}, u32[]{:S(2)}, u32[]{:S(2)}) %collective-permute-start.8) | collective-permute-done | bytes 524320 | tf_op jit(solution)/shard_map/ppermute | solution.py:30
  122.9 1.3 %put.1 = bf16[64,64,128]{2,1,0:T(8,128)(2,1)} custom-call(s32[5]{0:T(128)S(1)} %pad_add_fusion.refs_0_.place_ref, bf16[64,32,128]{2,1,0:T(8,128)(2,1)S(1)} %collective-permute-done.8.part_ref, bf16[64,64,128]{2,1,0:T(8,128)(2,1)} %get-tuple-element.20.whole_ref), custom_call_target="tpu_custom_call", output_to_operand_aliasing={{}: (2, {})} | custom-call | tf_op jit(solution)/shard_map/put/pallas_call | solution.py:252
  (4 shorter events, 0.0 us)
Async XLA Ops:
  0.0 66.8 %collective-permute-start.1 = (bf16[64,64,128]{2,1,0:T(8,128)(2,1)}, bf16[64,64,128]{2,1,0:T(8,128)(2,1)S(1)}, u32[]{:S(2)}, u32[]{:S(2)}) collective-permute-start(bf16[64,64,128]{2,1,0:T(8,128)(2,1)} %bitcast.26), channel_id=1, source_target_pairs={{0,64},{2,66},{4,68},{6,70},{8,72},{10,74},{12,76},{14,78},{16,80}... | collective-permute-start | bytes 3145736 | tf_op jit(solution)/shard_map/ppermute | solution.py:30
  6.7 30.1 %collective-permute-start = (bf16[400,128]{1,0:T(8,128)(2,1)}, bf16[400,128]{1,0:T(8,128)(2,1)S(1)}, u32[]{:S(2)}, u32[]{:S(2)}) collective-permute-start(bf16[400,128]{1,0:T(8,128)(2,1)} %get-tuple-element.13), channel_id=1, source_target_pairs={{0,64},{2,66},{4,68},{6,70},{8,72},{10,74},{12,76},{14,78},{16,80}... | collective-permute-start | bytes 307208 | tf_op jit(solution)/shard_map/ppermute | solution.py:30
  10.7 28.7 %collective-permute-start.3 = (bf16[384,128]{1,0:T(8,128)(2,1)}, bf16[384,128]{1,0:T(8,128)(2,1)S(1)}, u32[]{:S(2)}, u32[]{:S(2)}) collective-permute-start(bf16[384,128]{1,0:T(8,128)(2,1)} %get-tuple-element.14), channel_id=1, source_target_pairs={{0,66},{2,64},{4,70},{6,68},{8,74},{10,72},{12,78},{14,76},{16,82}... | collective-permute-start | bytes 294920 | tf_op jit(solution)/shard_map/ppermute | solution.py:30
  60.3 21.2 %collective-permute-start.4 = (bf16[3072,128]{1,0:T(8,128)(2,1)S(1)}, bf16[3072,128]{1,0:T(8,128)(2,1)S(1)}, u32[]{:S(2)}, u32[]{:S(2)}) collective-permute-start(bf16[3072,128]{1,0:T(8,128)(2,1)S(1)} %all_gather.3), channel_id=1, source_target_pairs={{0,16},{2,18},{4,20},{6,22},{8,24},{10,26},{12,28},{14,30},{16,32}... | collective-permute-start | bytes 2359304 | tf_op jit(solution)/shard_map/ppermute | solution.py:30
  63.5 20.9 %collective-permute-start.6 = (bf16[3072,128]{1,0:T(8,128)(2,1)S(1)}, bf16[3072,128]{1,0:T(8,128)(2,1)S(1)}, u32[]{:S(2)}, u32[]{:S(2)}) collective-permute-start(bf16[3072,128]{1,0:T(8,128)(2,1)S(1)} %all_gather.3), channel_id=1, source_target_pairs={{0,48},{2,50},{4,52},{6,54},{8,56},{10,58},{12,60},{14,62},{16,0},... | collective-permute-start | bytes 2359304 | tf_op jit(solution)/shard_map/ppermute | solution.py:30
  66.9 23.2 %collective-permute-start.2 = (bf16[64,64,128]{2,1,0:T(8,128)(2,1)S(1)}, bf16[64,64,128]{2,1,0:T(8,128)(2,1)S(1)}, u32[]{:S(2)}, u32[]{:S(2)}) collective-permute-start(bf16[64,64,128]{2,1,0:T(8,128)(2,1)S(1)} %collective-permute-done.1.refs_2_), channel_id=1, source_target_pairs={{0,2},{2,0},{4,6},{6,4},{8,10},{10,8},{12,14},{14,12},{16,18},{18,... | collective-permute-start | bytes 3145736 | tf_op jit(solution)/shard_map/ppermute | solution.py:30
  81.6 2.8 %copy-start = (bf16[3072,128]{1,0:T(8,128)(2,1)}, bf16[3072,128]{1,0:T(8,128)(2,1)S(1)}, u32[]{:S(2)}) copy-start(bf16[3072,128]{1,0:T(8,128)(2,1)S(1)} %collective-permute-done.4) | copy-start | bytes 2359300
  82.4 26.2 %collective-permute-start.5 = (bf16[1536,128]{1,0:T(8,128)(2,1)}, bf16[1536,128]{1,0:T(8,128)(2,1)S(1)}, u32[]{:S(2)}, u32[]{:S(2)}) collective-permute-start(bf16[1536,128]{1,0:T(8,128)(2,1)} %slice.18), channel_id=1, source_target_pairs={{0,16},{2,18},{4,20},{6,22},{8,24},{10,26},{12,28},{14,30},{16,32}... | collective-permute-start | bytes 1179656 | tf_op jit(solution)/shard_map/ppermute | solution.py:30
  84.4 1.1 copy-start.2
  85.4 23.3 %collective-permute-start.7 = (bf16[1536,128]{1,0:T(8,128)(2,1)}, bf16[1536,128]{1,0:T(8,128)(2,1)}, u32[]{:S(2)}, u32[]{:S(2)}) collective-permute-start(bf16[1536,128]{1,0:T(8,128)(2,1)} %slice.19), channel_id=1, source_target_pairs={{0,48},{2,50},{4,52},{6,54},{8,56},{10,58},{12,60},{14,62},{16,0},... | collective-permute-start | bytes 1179656 | tf_op jit(solution)/shard_map/ppermute | solution.py:30
  96.1 1.1 copy-start.1
  97.2 1.1 copy-start.3
  117.2 5.8 %collective-permute-start.8 = (bf16[64,32,128]{2,1,0:T(8,128)(2,1)S(1)}, bf16[64,32,128]{2,1,0:T(8,128)(2,1)S(1)}, u32[]{:S(2)}, u32[]{:S(2)}) collective-permute-start(bf16[64,32,128]{2,1,0:T(8,128)(2,1)S(1)} %get-tuple-element.19), channel_id=1, source_target_pairs={{0,2},{2,0},{4,6},{6,4},{8,10},{10,8},{12,14},{14,12},{16,18},{18,... | collective-permute-start | bytes 1572872 | tf_op jit(solution)/shard_map/ppermute | solution.py:30

commit v3 on v2

--- a/solution.py
+++ b/solution.py
@@ -235,7 +235,7 @@
             scratch_shapes=[pltpu.VMEM((keys, 2 * HD), jnp.bfloat16), pltpu.VMEM((keys, 2 * HD), jnp.bfloat16)],
         ),
         out_shape=out_shape,
-        compiler_params=pltpu.CompilerParams(vmem_limit_bytes=36 << 20),
+        compiler_params=pltpu.CompilerParams(vmem_limit_bytes=24 << 20),
         name="stage_last" if last else "stage",
     )(place, *operands)
 
@@ -283,15 +283,19 @@
     line = lax.all_gather(mine, "y", axis=0, tiled=True)
     parts = lambda a: a.reshape(-1, nc, 2, 2, cache + tok, width)
     half = line.shape[0] // 2
-    before = moved(line, sizes, dx=1)
-    after = moved(line, sizes, dx=-1)
-    state = stage(place, order, [q_own, q_other], [parts(line)], [(0, 0)], None, tok, cache)
-    far_a = moved(before[:half], sizes, dx=1)
-    far_b = moved(after[half:], sizes, dx=-1)
-    state = stage(place, order, [q_own, q_other], [parts(before), parts(after)], [(nx - 1, 0), (1, 0)], state, tok, cache)
-    final = [parts(far_a), parts(far_b)]
-    spots = [(2, 0), (2, ny // 2)]
-    result, theirs = stage(place, order, [q_own, q_other], final, spots, state, tok, cache, last=True, ahead=2)
+    low, high = line[:half], line[half:]
+    near_a = moved(low, sizes, dx=1)
+    near_b = moved(high, sizes, dx=-1)
+    rest_a = moved(high, sizes, dx=1)
+    rest_b = moved(low, sizes, dx=-1)
+    far_a = moved(near_a, sizes, dx=1)
+    far_b = moved(near_b, sizes, dx=-1)
+    mid = ny // 2
+    spots = [(0, 0), (nx - 1, 0), (1, mid)]
+    state = stage(place, order, [q_own, q_other], [parts(line), parts(near_a), parts(near_b)], spots, None, tok, cache)
+    chunks = [parts(rest_a), parts(rest_b), parts(far_a), parts(far_b)]
+    spots = [(nx - 1, mid), (1, 0), (2, 0), (2, mid)]
+    result, theirs = stage(place, order, [q_own, q_other], chunks, spots, state, tok, cache, last=True, ahead=2)
     theirs = moved(theirs, sizes, dc=1)
     return put(place, theirs, result)[None]
 

time: 125 us -> 115 us (0.920)
  waiting for transfers between devices: 36.4 us -> 28.8 us
  starting transfers between devices: 34.5 us -> 38.1 us
  local copies, waits for them, and re-layouts: 4.16 us -> 0.93 us
  Pallas kernels: 28 us -> 26 us
    ppermute x9 -> x11, waiting for transfers between devices: 36.4 us -> 28.8 us  [moved(): return lax.ppermute(value, FLAT, pairs)]
    ppermute x9 -> x11, starting transfers between devices: 34.5 us -> 38.1 us  [moved(): return lax.ppermute(value, FLAT, pairs)]
    unnamed x8 -> x0, local copies, waits for them, and re-layouts: 2.46 us -> none
    pallas_call x3 -> x2, Pallas kernels: 24.8 us -> 22.8 us  [stage(): pl.pallas_call(body, grid_spec=pltpu.PrefetchScalarGridSpec(num_scalar_pr...]
  transfers between devices with their start and end apart: 9 -> 11, of which waited for: 4 -> 6; matrix products, arithmetic and copies ran while one was open for 1% -> 1% of each run, Pallas kernels for 15% -> 11%
where the time goes in v3:
time: 115 us
  starting transfers between devices  38.1 us (33%)
  waiting for transfers between devices  28.8 us (25%)
  Pallas kernels  26 us (23%)
  blocking collectives  20.9 us (18%)
    ppermute x11, starting transfers between devices, moved(): return lax.ppermute(value, FLAT, pairs)  38.1 us
    ppermute x11, waiting for transfers between devices, moved(): return lax.ppermute(value, FLAT, pairs)  28.8 us
    pallas_call x2, Pallas kernels, stage(): pl.pallas_call(body, grid_spec=pltpu.PrefetchScalarGridSpec(num_scalar_pr...  22.8 us
    all_gather x1, blocking collectives, relay(): line = lax.all_gather(mine, 'y', axis=0, tiled=True)  20.9 us
  transfers between devices with their start and end apart: 11, of which 6 were waited for; matrix products, arithmetic and copies ran while one was open for 1% of the time, Pallas kernels for 11%

profile of v3, /device:TPU:1, one launch (start us, length us, event | category | flops | bytes accessed | tf_op | source)
XLA Modules:
  0.0 114.9 jit_solution(135651557695143869)
XLA Ops:
  0.0 4.8 %collective-permute-start.1 = (bf16[64,64,128]{2,1,0:T(8,128)(2,1)}, bf16[64,64,128]{2,1,0:T(8,128)(2,1)S(1)}, u32[]{:S(2)}, u32[]{:S(2)}) collective-permute-start(bf16[64,64,128]{2,1,0:T(8,128)(2,1)} %bitcast.26), channel_id=1, source_target_pairs={{0,64},{2,66},{4,68},{6,70},{8,72},{10,74},{12,76},{14,78},{16,80}... | collective-permute-start | bytes 3145736 | tf_op jit(solution)/shard_map/ppermute | solution.py:30
  4.8 1.8 %pack_kv.1 = (bf16[400,128]{1,0:T(8,128)(2,1)}, bf16[384,128]{1,0:T(8,128)(2,1)}) custom-call(s32[1]{0:T(128)} %bitcast.2.core_ref, s32[2,2,4]{2,1,0:T(2,128)} %bitcast.25, s32[1,64]{1,0:T(1,128)} %order_ref.1, bf16[256,128]{1,0:T(8,128)(2,1)} %bitcast.21, bf16[256,128]{1,0:T(8,128)(2,1)} %bitcast.22, bf16[128,128]{1,0:T(8,128)(2,1)} %bitcast.23, ...), custom_call_target="tpu_custom_call" | custom-call | tf_op jit(solution)/shard_map/pack_kv/pallas_call | solution.py:84
  6.7 4.0 %collective-permute-start = (bf16[400,128]{1,0:T(8,128)(2,1)}, bf16[400,128]{1,0:T(8,128)(2,1)S(1)}, u32[]{:S(2)}, u32[]{:S(2)}) collective-permute-start(bf16[400,128]{1,0:T(8,128)(2,1)} %get-tuple-element.11), channel_id=1, source_target_pairs={{0,64},{2,66},{4,68},{6,70},{8,72},{10,74},{12,76},{14,78},{16,80}... | collective-permute-start | bytes 307208 | tf_op jit(solution)/shard_map/ppermute | solution.py:30
  10.7 5.1 %collective-permute-start.3 = (bf16[384,128]{1,0:T(8,128)(2,1)}, bf16[384,128]{1,0:T(8,128)(2,1)S(1)}, u32[]{:S(2)}, u32[]{:S(2)}) collective-permute-start(bf16[384,128]{1,0:T(8,128)(2,1)} %get-tuple-element.12), channel_id=1, source_target_pairs={{0,66},{2,64},{4,70},{6,68},{8,74},{10,72},{12,78},{14,76},{16,82}... | collective-permute-start | bytes 294920 | tf_op jit(solution)/shard_map/ppermute | solution.py:30
  15.8 20.9 %collective-permute-done = bf16[400,128]{1,0:T(8,128)(2,1)S(1)} collective-permute-done((bf16[400,128]{1,0:T(8,128)(2,1)}, bf16[400,128]{1,0:T(8,128)(2,1)S(1)}, u32[]{:S(2)}, u32[]{:S(2)}) %collective-permute-start) | collective-permute-done | bytes 102432 | tf_op jit(solution)/shard_map/ppermute | solution.py:30
  36.7 2.7 %collective-permute-done.3 = bf16[384,128]{1,0:T(8,128)(2,1)S(1)} collective-permute-done((bf16[384,128]{1,0:T(8,128)(2,1)}, bf16[384,128]{1,0:T(8,128)(2,1)S(1)}, u32[]{:S(2)}, u32[]{:S(2)}) %collective-permute-start.3) | collective-permute-done | bytes 98336 | tf_op jit(solution)/shard_map/ppermute | solution.py:30
  39.4 20.9 %all_gather.3 = bf16[3072,128]{1,0:T(8,128)(2,1)S(1)} all-gather(bf16[768,128]{1,0:T(8,128)(2,1)S(1)} %pad_maximum_fusion), channel_id=1, replica_groups=mesh['pipe'=8,'x'=4,'y'=4,'core'=2,'tp'=2] {'y'}, dimensions={0}, use_global_device_ids=true | all-gather | bytes 983040 | tf_op jit(solution)/shard_map/all_gather | solution.py:283
  60.3 0.0 collective-permute-done.1.refs_2_
  60.3 2.8 %collective-permute-start.2 = (bf16[64,64,128]{2,1,0:T(8,128)(2,1)S(1)}, bf16[64,64,128]{2,1,0:T(8,128)(2,1)S(1)}, u32[]{:S(2)}, u32[]{:S(2)}) collective-permute-start(bf16[64,64,128]{2,1,0:T(8,128)(2,1)S(1)} %collective-permute-done.1.refs_2_), channel_id=1, source_target_pairs={{0,2},{2,0},{4,6},{6,4},{8,10},{10,8},{12,14},{14,12},{16,18},{18,... | collective-permute-start | bytes 3145736 | tf_op jit(solution)/shard_map/ppermute | solution.py:30
  63.2 0.9 fusion
  64.1 3.1 %collective-permute-start.6 = (bf16[1536,128]{1,0:T(8,128)(2,1)}, bf16[1536,128]{1,0:T(8,128)(2,1)}, u32[]{:S(2)}, u32[]{:S(2)}) collective-permute-start(bf16[1536,128]{1,0:T(8,128)(2,1)} %get-tuple-element.17), channel_id=1, source_target_pairs={{0,16},{2,18},{4,20},{6,22},{8,24},{10,26},{12,28},{14,30},{16,32}... | collective-permute-start | bytes 1179656 | tf_op jit(solution)/shard_map/ppermute | solution.py:30
  67.2 3.4 %collective-permute-start.8 = (bf16[1536,128]{1,0:T(8,128)(2,1)}, bf16[1536,128]{1,0:T(8,128)(2,1)}, u32[]{:S(2)}, u32[]{:S(2)}) collective-permute-start(bf16[1536,128]{1,0:T(8,128)(2,1)} %get-tuple-element.18), channel_id=1, source_target_pairs={{0,48},{2,50},{4,52},{6,54},{8,56},{10,58},{12,60},{14,62},{16,0},... | collective-permute-start | bytes 1179656 | tf_op jit(solution)/shard_map/ppermute | solution.py:30
  70.6 3.2 %collective-permute-start.5 = (bf16[1536,128]{1,0:T(8,128)(2,1)}, bf16[1536,128]{1,0:T(8,128)(2,1)S(1)}, u32[]{:S(2)}, u32[]{:S(2)}) collective-permute-start(bf16[1536,128]{1,0:T(8,128)(2,1)} %get-tuple-element.17), channel_id=1, source_target_pairs={{0,48},{2,50},{4,52},{6,54},{8,56},{10,58},{12,60},{14,62},{16,0},... | collective-permute-start | bytes 1179656 | tf_op jit(solution)/shard_map/ppermute | solution.py:30
  73.8 2.1 %collective-permute-start.4 = (bf16[1536,128]{1,0:T(8,128)(2,1)}, bf16[1536,128]{1,0:T(8,128)(2,1)}, u32[]{:S(2)}, u32[]{:S(2)}) collective-permute-start(bf16[1536,128]{1,0:T(8,128)(2,1)} %get-tuple-element.18), channel_id=1, source_target_pairs={{0,16},{2,18},{4,20},{6,22},{8,24},{10,26},{12,28},{14,30},{16,32}... | collective-permute-start | bytes 1179656 | tf_op jit(solution)/shard_map/ppermute | solution.py:30
  75.9 2.3 %collective-permute-done.6 = bf16[1536,128]{1,0:T(8,128)(2,1)} collective-permute-done((bf16[1536,128]{1,0:T(8,128)(2,1)}, bf16[1536,128]{1,0:T(8,128)(2,1)}, u32[]{:S(2)}, u32[]{:S(2)}) %collective-permute-start.6) | collective-permute-done | bytes 393248 | tf_op jit(solution)/shard_map/ppermute | solution.py:30
  78.2 1.9 %collective-permute-start.7 = (bf16[1536,128]{1,0:T(8,128)(2,1)}, bf16[1536,128]{1,0:T(8,128)(2,1)}, u32[]{:S(2)}, u32[]{:S(2)}) collective-permute-start(bf16[1536,128]{1,0:T(8,128)(2,1)} %collective-permute-done.6), channel_id=1, source_target_pairs={{0,16},{2,18},{4,20},{6,22},{8,24},{10,26},{12,28},{14,30},{16,32}... | collective-permute-start | bytes 1179656 | tf_op jit(solution)/shard_map/ppermute | solution.py:30
  80.1 0.0 collective-permute-done.8
  80.1 4.6 %collective-permute-start.9 = (bf16[1536,128]{1,0:T(8,128)(2,1)}, bf16[1536,128]{1,0:T(8,128)(2,1)}, u32[]{:S(2)}, u32[]{:S(2)}) collective-permute-start(bf16[1536,128]{1,0:T(8,128)(2,1)} %collective-permute-done.8), channel_id=1, source_target_pairs={{0,48},{2,50},{4,52},{6,54},{8,56},{10,58},{12,60},{14,62},{16,0},... | collective-permute-start | bytes 1179656 | tf_op jit(solution)/shard_map/ppermute | solution.py:30
  84.7 0.1 pad_add_fusion.refs_0_.place_ref
  84.8 0.0 collective-permute-done.2.refs_3_
  84.8 10.5 %stage.1 = (f32[2,2048,256]{2,1,0:T(8,128)S(1)}, f32[2,2048,128]{2,1,0:T(8,128)S(1)}) custom-call(s32[5]{0:T(128)S(1)} %pad_add_fusion.refs_0_.place_ref, s32[1,64]{1,0:T(1,128)S(1)} %slice_convert_fusion.refs_1_, bf16[64,64,128]{2,1,0:T(8,128)(2,1)S(1)} %collective-permute-done.1.refs_2_, bf16[64,64,128]{2,1,0:T(8,128)(2,1)S(1)} %collective-permute-done.2.refs_3_, ...), custom_call_target="tpu_custom_call" | custom-call | tf_op jit(solution)/shard_map/stage/pallas_call | solution.py:228
  95.3 0.0 collective-permute-done.5
  95.3 0.0 collective-permute-done.4
  95.3 0.2 collective-permute-done.7
  95.5 1.2 %collective-permute-done.9 = bf16[1536,128]{1,0:T(8,128)(2,1)} collective-permute-done((bf16[1536,128]{1,0:T(8,128)(2,1)}, bf16[1536,128]{1,0:T(8,128)(2,1)}, u32[]{:S(2)}, u32[]{:S(2)}) %collective-permute-start.9) | collective-permute-done | bytes 393248 | tf_op jit(solution)/shard_map/ppermute | solution.py:30
  96.7 12.3 %stage_last.1 = (bf16[64,64,128]{2,1,0:T(8,128)(2,1)}, bf16[64,32,128]{2,1,0:T(8,128)(2,1)S(1)}) custom-call(s32[5]{0:T(128)S(1)} %pad_add_fusion.refs_0_.place_ref, s32[1,64]{1,0:T(1,128)S(1)} %slice_convert_fusion.refs_1_, bf16[64,64,128]{2,1,0:T(8,128)(2,1)S(1)} %collective-permute-done.1.refs_2_, ...), custom_call_target="tpu_custom_call" | custom-call | tf_op jit(solution)/shard_map/stage_last/pallas_call | solution.py:228
  109.0 3.0 %collective-permute-start.10 = (bf16[64,32,128]{2,1,0:T(8,128)(2,1)S(1)}, bf16[64,32,128]{2,1,0:T(8,128)(2,1)S(1)}, u32[]{:S(2)}, u32[]{:S(2)}) collective-permute-start(bf16[64,32,128]{2,1,0:T(8,128)(2,1)S(1)} %get-tuple-element.15), channel_id=1, source_target_pairs={{0,2},{2,0},{4,6},{6,4},{8,10},{10,8},{12,14},{14,12},{16,18},{18,... | collective-permute-start | bytes 1572872 | tf_op jit(solution)/shard_map/ppermute | solution.py:30
  112.1 1.5 %collective-permute-done.10.part_ref = bf16[64,32,128]{2,1,0:T(8,128)(2,1)S(1)} collective-permute-done((bf16[64,32,128]{2,1,0:T(8,128)(2,1)S(1)}, bf16[64,32,128]{2,1,0:T(8,128)(2,1)S(1)}, u32[]{:S(2)}, u32[]{:S(2)}) %collective-permute-start.10) | collective-permute-done | bytes 524320 | tf_op jit(solution)/shard_map/ppermute | solution.py:30
  113.6 1.3 %put.1 = bf16[64,64,128]{2,1,0:T(8,128)(2,1)} custom-call(s32[5]{0:T(128)S(1)} %pad_add_fusion.refs_0_.place_ref, bf16[64,32,128]{2,1,0:T(8,128)(2,1)S(1)} %collective-permute-done.10.part_ref, bf16[64,64,128]{2,1,0:T(8,128)(2,1)} %get-tuple-element.16.whole_ref), custom_call_target="tpu_custom_call", output_to_operand_aliasing={{}: (2, {})} | custom-call | tf_op jit(solution)/shard_map/put/pallas_call | solution.py:252
  (4 shorter events, 0.0 us)
Async XLA Ops:
  0.0 60.3 %collective-permute-start.1 = (bf16[64,64,128]{2,1,0:T(8,128)(2,1)}, bf16[64,64,128]{2,1,0:T(8,128)(2,1)S(1)}, u32[]{:S(2)}, u32[]{:S(2)}) collective-permute-start(bf16[64,64,128]{2,1,0:T(8,128)(2,1)} %bitcast.26), channel_id=1, source_target_pairs={{0,64},{2,66},{4,68},{6,70},{8,72},{10,74},{12,76},{14,78},{16,80}... | collective-permute-start | bytes 3145736 | tf_op jit(solution)/shard_map/ppermute | solution.py:30
  6.7 30.1 %collective-permute-start = (bf16[400,128]{1,0:T(8,128)(2,1)}, bf16[400,128]{1,0:T(8,128)(2,1)S(1)}, u32[]{:S(2)}, u32[]{:S(2)}) collective-permute-start(bf16[400,128]{1,0:T(8,128)(2,1)} %get-tuple-element.11), channel_id=1, source_target_pairs={{0,64},{2,66},{4,68},{6,70},{8,72},{10,74},{12,76},{14,78},{16,80}... | collective-permute-start | bytes 307208 | tf_op jit(solution)/shard_map/ppermute | solution.py:30
  10.7 28.7 %collective-permute-start.3 = (bf16[384,128]{1,0:T(8,128)(2,1)}, bf16[384,128]{1,0:T(8,128)(2,1)S(1)}, u32[]{:S(2)}, u32[]{:S(2)}) collective-permute-start(bf16[384,128]{1,0:T(8,128)(2,1)} %get-tuple-element.12), channel_id=1, source_target_pairs={{0,66},{2,64},{4,70},{6,68},{8,74},{10,72},{12,78},{14,76},{16,82}... | collective-permute-start | bytes 294920 | tf_op jit(solution)/shard_map/ppermute | solution.py:30
  60.3 24.5 %collective-permute-start.2 = (bf16[64,64,128]{2,1,0:T(8,128)(2,1)S(1)}, bf16[64,64,128]{2,1,0:T(8,128)(2,1)S(1)}, u32[]{:S(2)}, u32[]{:S(2)}) collective-permute-start(bf16[64,64,128]{2,1,0:T(8,128)(2,1)S(1)} %collective-permute-done.1.refs_2_), channel_id=1, source_target_pairs={{0,2},{2,0},{4,6},{6,4},{8,10},{10,8},{12,14},{14,12},{16,18},{18,... | collective-permute-start | bytes 3145736 | tf_op jit(solution)/shard_map/ppermute | solution.py:30
  64.1 14.1 %collective-permute-start.6 = (bf16[1536,128]{1,0:T(8,128)(2,1)}, bf16[1536,128]{1,0:T(8,128)(2,1)}, u32[]{:S(2)}, u32[]{:S(2)}) collective-permute-start(bf16[1536,128]{1,0:T(8,128)(2,1)} %get-tuple-element.17), channel_id=1, source_target_pairs={{0,16},{2,18},{4,20},{6,22},{8,24},{10,26},{12,28},{14,30},{16,32}... | collective-permute-start | bytes 1179656 | tf_op jit(solution)/shard_map/ppermute | solution.py:30
  67.2 12.9 %collective-permute-start.8 = (bf16[1536,128]{1,0:T(8,128)(2,1)}, bf16[1536,128]{1,0:T(8,128)(2,1)}, u32[]{:S(2)}, u32[]{:S(2)}) collective-permute-start(bf16[1536,128]{1,0:T(8,128)(2,1)} %get-tuple-element.18), channel_id=1, source_target_pairs={{0,48},{2,50},{4,52},{6,54},{8,56},{10,58},{12,60},{14,62},{16,0},... | collective-permute-start | bytes 1179656 | tf_op jit(solution)/shard_map/ppermute | solution.py:30
  70.6 24.7 %collective-permute-start.5 = (bf16[1536,128]{1,0:T(8,128)(2,1)}, bf16[1536,128]{1,0:T(8,128)(2,1)S(1)}, u32[]{:S(2)}, u32[]{:S(2)}) collective-permute-start(bf16[1536,128]{1,0:T(8,128)(2,1)} %get-tuple-element.17), channel_id=1, source_target_pairs={{0,48},{2,50},{4,52},{6,54},{8,56},{10,58},{12,60},{14,62},{16,0},... | collective-permute-start | bytes 1179656 | tf_op jit(solution)/shard_map/ppermute | solution.py:30
  73.8 21.5 %collective-permute-start.4 = (bf16[1536,128]{1,0:T(8,128)(2,1)}, bf16[1536,128]{1,0:T(8,128)(2,1)}, u32[]{:S(2)}, u32[]{:S(2)}) collective-permute-start(bf16[1536,128]{1,0:T(8,128)(2,1)} %get-tuple-element.18), channel_id=1, source_target_pairs={{0,16},{2,18},{4,20},{6,22},{8,24},{10,26},{12,28},{14,30},{16,32}... | collective-permute-start | bytes 1179656 | tf_op jit(solution)/shard_map/ppermute | solution.py:30
  78.2 17.3 %collective-permute-start.7 = (bf16[1536,128]{1,0:T(8,128)(2,1)}, bf16[1536,128]{1,0:T(8,128)(2,1)}, u32[]{:S(2)}, u32[]{:S(2)}) collective-permute-start(bf16[1536,128]{1,0:T(8,128)(2,1)} %collective-permute-done.6), channel_id=1, source_target_pairs={{0,16},{2,18},{4,20},{6,22},{8,24},{10,26},{12,28},{14,30},{16,32}... | collective-permute-start | bytes 1179656 | tf_op jit(solution)/shard_map/ppermute | solution.py:30
  80.1 16.6 %collective-permute-start.9 = (bf16[1536,128]{1,0:T(8,128)(2,1)}, bf16[1536,128]{1,0:T(8,128)(2,1)}, u32[]{:S(2)}, u32[]{:S(2)}) collective-permute-start(bf16[1536,128]{1,0:T(8,128)(2,1)} %collective-permute-done.8), channel_id=1, source_target_pairs={{0,48},{2,50},{4,52},{6,54},{8,56},{10,58},{12,60},{14,62},{16,0},... | collective-permute-start | bytes 1179656 | tf_op jit(solution)/shard_map/ppermute | solution.py:30
  109.0 4.6 %collective-permute-start.10 = (bf16[64,32,128]{2,1,0:T(8,128)(2,1)S(1)}, bf16[64,32,128]{2,1,0:T(8,128)(2,1)S(1)}, u32[]{:S(2)}, u32[]{:S(2)}) collective-permute-start(bf16[64,32,128]{2,1,0:T(8,128)(2,1)S(1)} %get-tuple-element.15), channel_id=1, source_target_pairs={{0,2},{2,0},{4,6},{6,4},{8,10},{10,8},{12,14},{14,12},{16,18},{18,... | collective-permute-start | bytes 1572872 | tf_op jit(solution)/shard_map/ppermute | solution.py:30
